TPU v7x, 32 devices: a whole 2x2x4 slice. The times are simulated.
32 devices in a mesh: grp: 4 (over z), gx: 2 (over y), gy: 4 (over x, core).
Axes of the slice: x: 2, y: 2, z: 4, core: 2. Of those that a mesh axis runs over, the one named last changes fastest.
Arguments:
- checkpoint: float32 [2, 2, 2, 32, 64, 256], P(None, None, None, 'gx', 'gy'), may hold values from -6 to 6
- courant: float32 [32, 64, 256], P('gx', 'gy'), may hold values from 0.03 to 0.15
- epsilon: float32 [32, 64, 256], P('gx', 'gy'), may hold values from 0.3 to 0.6
- delta: float32 [32, 64, 256], P('gx', 'gy'), may hold values from 0.05 to 0.3
- positions: int32 [4, 3, 512], replicated, may hold values from 0 to 255, as said below
- amplitudes: float32 [4, 16, 512], replicated, may hold values from -6 to 6
- offsets: int32 [16], replicated, may hold values from -8 to 8, as said below
Outputs:
- image: float32 [16, 32, 64, 256], P('grp', 'gx', 'gy')
Inputs may be any that keep to these rules, and one draw needn't show every extreme that they name: `positions`: each column of a row is a cell inside the grid: x below 32, y below 64, z below 256. `offsets`: both -8 and 8 occur.
All inputs are finite; a program needn't handle non-finite values.
Results may differ from a plain program's by a relative error of at most 0.0003.
Values sent between devices are 32-bit elements; how exact they have to be, the bound alone decides.
A program may use at most 128 MiB of HBM per device.

v0:
```python
import functools
import math
import jax
import jax.numpy as jnp
from jax import lax
from jax.experimental import pallas as pl
from jax.experimental.pallas import tpu as pltpu
from jax.sharding import PartitionSpec as P

SNAP = 4
HMAX = 8
MESH = pl.DeviceIdType.MESH


def kernel(sizes, courant, epsilon, delta, checkpoint, positions, amplitudes, offsets, gathered,
           state, hor, cpl, ver, edge, inj, pick, spot, snaps, image, outgoing, hx, hy, sy,
           hs, hr, ss, sr, gs, gr):
    ng, nx, ny = sizes
    shots = checkpoint.shape[0]
    tx, ty, nz = courant.shape
    nrec = positions.shape[2]
    blocks = amplitudes.shape[1] // SNAP
    nh = offsets.shape[0]
    own = nh // ng
    qy = ty // ng
    sub = shots * qy
    groups = tx // qy
    g, a, b = lax.axis_index("grp"), lax.axis_index("gx"), lax.axis_index("gy")
    flip = b % 2
    sign = 1 - 2 * flip
    q = g + flip * (ng - 1 - 2 * g)

    inner_lo, inner_hi = (q > 0).astype(jnp.int32), (q < ng - 1).astype(jnp.int32)
    sides = (
        (a > 0, {"grp": g, "gx": a - 1, "gy": b}),
        (a < nx - 1, {"grp": g, "gx": a + 1, "gy": b}),
        ((q > 0) | (b > 0), {"grp": g - sign * inner_lo, "gx": a, "gy": b - 1 + inner_lo}),
        ((q < ng - 1) | (b < ny - 1), {"grp": g + sign * inner_hi, "gx": a, "gy": b + 1 - inner_hi}),
    )

    barrier = pltpu.get_barrier_semaphore()
    for there, device in sides:
        @pl.when(there)
        def _(device=device):
            pl.semaphore_signal(barrier, inc=1, device_id=device, device_id_type=MESH)
    for step in range(1, ng):
        pl.semaphore_signal(
            barrier, inc=1, device_id={"grp": (g + step) % ng, "gx": a, "gy": b}, device_id_type=MESH
        )

    rows = lax.broadcasted_iota(jnp.int32, (sub, nz), 0)
    lanes = lax.broadcasted_iota(jnp.int32, (sub, nz), 1)
    place = rows % qy
    is_odd = rows * 0 + q % 2 == 1
    first = rows < qy
    half = pl.ds(pl.multiple_of((q // 2) * sub, sub), sub)

    def turn(v, shift, axis=0):
        shift = shift % v.shape[axis]
        return v if shift == 0 else pltpu.roll(v, shift, axis)

    def low(v):
        return jnp.where(is_odd, turn(v, qy), v)

    def high(v):
        return jnp.where(is_odd, v, turn(v, qy))

    def both(v):
        return jnp.where(first, low(v), high(v))

    zero = jnp.zeros((sub, nz), jnp.float32)

    def prepare(x, carry):
        c, e, d = both(courant[x, half, :]), both(epsilon[x, half, :]), both(delta[x, half, :])
        hor[x] = c + 2.0 * c * e
        cpl[x] = c * jnp.sqrt(2.0 * d + 1.0)
        ver[x] = c
        for moment in range(2):
            for field in range(2):
                state[moment, field, 0, x] = jnp.where(
                    first, low(checkpoint[0, moment, field, x, half, :]), high(checkpoint[1, moment, field, x, half, :])
                )
                state[moment, field, 1, x] = zero
        return carry

    lax.fori_loop(0, tx, prepare, 0)

    def pack(side, r, slot, source):
        for m in range(groups):
            packed = None
            for i in range(qy):
                tile = turn(source(m * qy + i), i if side == 0 else i - (qy - 1))
                packed = tile if packed is None else jnp.where(place == i, tile, packed)
            sy[slot, side, r, m] = packed

    for r in range(2):
        for side in range(2):
            pack(side, r, 0, lambda x: state[0, 0, r, x])

    for side in range(2):
        for slot in range(2):
            @pl.when(jnp.logical_not(sides[side][0]))
            def _(slot=slot, side=side):
                hx[slot, side] = jnp.zeros(hx.shape[2:], jnp.float32)

            @pl.when(jnp.logical_not(sides[2 + side][0]))
            def _(slot=slot, side=side):
                hy[slot, side] = jnp.zeros(hy.shape[2:], jnp.float32)

    total = ng - 1
    for there, _ in sides:
        total = total + there.astype(jnp.int32)
    pl.semaphore_wait(barrier, total)

    def halo_copy(slot, r, side):
        if side < 2:
            source, target = state.at[slot, 0, r, 0 if side == 0 else tx - 1], hx.at[slot, 1 - side, r]
        else:
            source, target = sy.at[slot, side - 2, r], hy.at[slot, 3 - side, r]
        return pltpu.make_async_remote_copy(
            src_ref=source, dst_ref=target, send_sem=hs.at[slot, r, side], recv_sem=hr.at[slot, r, side ^ 1],
            device_id=sides[side][1], device_id_type=MESH,
        )

    def halo_arrival(slot, r, side):
        target = hx.at[slot, side, r] if side < 2 else hy.at[slot, side - 2, r]
        return pltpu.make_async_remote_copy(
            src_ref=target, dst_ref=target, send_sem=hs.at[slot, r, side], recv_sem=hr.at[slot, r, side],
            device_id=sides[side][1], device_id_type=MESH,
        )

    def snap_copy(j, r, side, arrival=False):
        source = pl.ds(HMAX, HMAX) if side == 0 else pl.ds(tx, HMAX)
        target = pl.ds(HMAX + tx, HMAX) if side == 0 else pl.ds(0, HMAX)
        if arrival:
            source = target = pl.ds(0, HMAX) if side == 0 else pl.ds(HMAX + tx, HMAX)
        return pltpu.make_async_remote_copy(
            src_ref=snaps.at[j, r, source], dst_ref=snaps.at[j, r, target], send_sem=ss.at[j, r, side],
            recv_sem=sr.at[j, r, side if arrival else side ^ 1], device_id=sides[side][1], device_id_type=MESH,
        )

    def send_halos(slot, r):
        for side in (2, 3, 0, 1):
            @pl.when(sides[side][0])
            def _(side=side):
                halo_copy(slot, r, side).start()

    def wait_halos(slot, r):
        for side in range(4):
            @pl.when(sides[side][0])
            def _(side=side):
                halo_arrival(slot, r, side).wait_recv()
                halo_copy(slot, r, side).wait_send()

    def send_snap(j, r):
        for side in range(2):
            @pl.when(sides[side][0])
            def _(side=side):
                snap_copy(j, r, side).start()

    def wait_snap(j):
        for r in range(2):
            for side in range(2):
                @pl.when(sides[side][0])
                def _(r=r, side=side):
                    snap_copy(j, r, side, True).wait_recv()
                    snap_copy(j, r, side).wait_send()

    send_halos(0, 0)
    send_halos(0, 1)

    column = lax.broadcasted_iota(jnp.int32, (tx * sub, nrec), 0)
    level = lax.broadcasted_iota(jnp.int32, (nz, nrec), 0)
    for r in range(2):
        for s in range(shots):
            px = positions[0, 2 * s + r : 2 * s + r + 1, :] - a * tx
            py = positions[1, 2 * s + r : 2 * s + r + 1, :] - (b * ty + q * qy)
            pz = positions[2, 2 * s + r : 2 * s + r + 1, :]
            inside = (px >= 0) & (px < tx) & (py >= 0) & (py < qy)
            cell = jnp.where(inside, px * sub + s * qy + py, -1)
            points = pl.ds(s * nrec, nrec)
            pick[r, :, points] = jnp.where(column == cell, 1.0, 0.0).astype(jnp.bfloat16)
            spot[r, points, :] = jnp.where(level == pz, 1.0, 0.0).T.astype(jnp.bfloat16)

    def clear(k, carry):
        for x in range(tx):
            image[k, x] = zero
        return carry

    lax.fori_loop(0, nh, clear, 0)
    for side in range(2):
        @pl.when(jnp.logical_not(sides[side][0]))
        def _(side=side):
            def blank(j, carry):
                for r in range(2):
                    for x in range(HMAX):
                        snaps[j, r, side * (HMAX + tx) + x] = zero
                return carry

            lax.fori_loop(0, blocks, blank, 0)

    def inject(moment, r):
        strength = jnp.concatenate(
            [amplitudes[2 * s + r, pl.ds(moment, 1), :] for s in range(shots)], axis=1
        )
        strength = jnp.broadcast_to(strength, (2 * sub, shots * nrec))
        upper = strength.astype(jnp.bfloat16)
        lower = (strength - upper.astype(jnp.float32)).astype(jnp.bfloat16)
        spread = jnp.concatenate(
            [
                pick[r, pl.ds(2 * sub * m, 2 * sub), :] * part
                for part in (upper, lower)
                for m in range(tx // 2)
            ],
            axis=0,
        )
        found = jnp.dot(spread, spot[r], preferred_element_type=jnp.float32)
        inj[r] = found[: tx * sub] + found[tx * sub :]

    def advance(p, r):
        for x in range(tx):
            m, w = state[p, 0, r, x], state[p, 1, r, x]
            across = (
                jnp.where(place == 0, 0.0, turn(m, 1))
                + jnp.where(place == qy - 1, 0.0, turn(m, -1))
                - 4.0 * m
            )
            if x > 0:
                across = across + state[p, 0, r, x - 1]
            if x < tx - 1:
                across = across + state[p, 0, r, x + 1]
            down = (
                jnp.where(lanes == 0, 0.0, turn(w, 1, 1))
                + jnp.where(lanes == nz - 1, 0.0, turn(w, -1, 1))
                - 2.0 * w
            )
            source = inj[r, pl.ds(x * sub, sub), :]
            coupling = cpl[x]
            state[1 - p, 0, r, x] = 2.0 * m - state[1 - p, 0, r, x] + hor[x] * across + coupling * down + source
            state[1 - p, 1, r, x] = 2.0 * w - state[1 - p, 1, r, x] + coupling * across + ver[x] * down + source

    def repair(p, r, j):
        for m in range(groups):
            below, above = hy[p, 0, r, m], hy[p, 1, r, m]
            packed = [None, None]
            for i in range(qy):
                x = m * qy + i
                extra = jnp.where(place == 0, turn(below, -i), 0.0)
                extra = jnp.where(place == qy - 1, turn(above, qy - 1 - i), extra)
                if x == 0:
                    extra = extra + hx[p, 0, r]
                if x == tx - 1:
                    extra = extra + hx[p, 1, r]
                main = state[1 - p, 0, r, x] + hor[x] * extra
                state[1 - p, 0, r, x] = main
                edge[x] = extra
                for side in range(2):
                    tile = turn(main, i if side == 0 else i - (qy - 1))
                    packed[side] = tile if i == 0 else jnp.where(place == i, tile, packed[side])
                if j is not None:
                    snaps[j, r, HMAX + x] = main
            for side in range(2):
                sy[1 - p, side, r, m] = packed[side]

    def repair_aux(p, r):
        for x in range(tx):
            state[1 - p, 1, r, x] = state[1 - p, 1, r, x] + cpl[x] * edge[x]

    def correlate(j):
        def one(k, carry):
            shift = offsets[k]
            for x in range(tx):
                image[k, x] = image[k, x] + snaps[j, 0, HMAX - shift + x] * snaps[j, 1, HMAX + shift + x]
            return carry

        lax.fori_loop(0, nh, one, 0)

    def block(j, carry):
        for i in range(SNAP):
            p = i % 2
            for r in range(2):
                inject(j * SNAP + i, r)
                advance(p, r)
                if i == 2 and r == 0:
                    @pl.when(j > 0)
                    def _():
                        wait_snap(j - 1)
                        correlate(j - 1)
                wait_halos(p, r)
                repair(p, r, j if i == SNAP - 1 else None)
                if i == SNAP - 1:
                    @pl.when(j < blocks - 1)
                    def _():
                        send_halos(1 - p, r)

                    @pl.when(j == blocks - 1)
                    def _():
                        send_snap(j, r)
                else:
                    send_halos(1 - p, r)
                if i == 0:
                    @pl.when(j > 0)
                    def _():
                        send_snap(j - 1, r)
                repair_aux(p, r)
        return carry

    lax.fori_loop(0, blocks, block, 0)
    wait_snap(blocks - 1)

    def peer_copy(d, arrival=False):
        return pltpu.make_async_remote_copy(
            src_ref=outgoing.at[d], dst_ref=gathered.at[d if arrival else g], send_sem=gs.at[d],
            recv_sem=gr.at[d if arrival else g],
            device_id={"grp": d, "gx": a, "gy": b}, device_id_type=MESH,
        )

    def finish(d, target):
        def pair(n, carry):
            for x in range(tx):
                tiles = []
                for c in range(2):
                    k = d * own + 2 * n + c
                    shift = offsets[k]
                    tile = image[k, x] + snaps[blocks - 1, 0, HMAX - shift + x] * snaps[blocks - 1, 1, HMAX + shift + x]
                    tiles.append(tile + turn(tile, qy))
                target[n, x] = jnp.where(first, tiles[0], tiles[1])
            return carry

        lax.fori_loop(0, own // 2, pair, 0)

    for step in range(1, ng):
        d = (g + step) % ng
        finish(d, outgoing.at[d])
        peer_copy(d).start()
    finish(g, gathered.at[g])
    for step in range(1, ng):
        d = (g + step) % ng
        peer_copy(d, True).wait_recv()
        peer_copy(d).wait_send()


def place(gathered, out):
    ng, pairs, span, sub, nz = gathered.shape
    flip = lax.axis_index("gy") % 2
    qy = sub // 2
    first = lax.broadcasted_iota(jnp.int32, (sub, nz), 0) < qy
    for h in range(ng // 2):
        left, right = 2 * h, 2 * h + 1
        one = left + flip * (ng - 1 - 2 * left)
        two = right + flip * (ng - 1 - 2 * right)
        for n in range(pairs):
            for x in range(span):
                u, v = gathered[one, n, x], gathered[two, n, x]
                out[2 * n, x, pl.ds(h * sub, sub), :] = jnp.where(first, u, pltpu.roll(v, qy, 0))
                out[2 * n + 1, x, pl.ds(h * sub, sub), :] = jnp.where(first, pltpu.roll(u, qy, 0), v)


def shards(sizes, checkpoint, courant, epsilon, delta, positions, amplitudes, offsets):
    ng, nx, ny = sizes
    shots = checkpoint.shape[0]
    tx, ty, nz = courant.shape
    nrec = positions.shape[2]
    blocks = amplitudes.shape[1] // SNAP
    nh = offsets.shape[0]
    own = nh // ng
    qy = ty // ng
    sub = shots * qy
    groups = tx // qy
    assert shots == 2 and sub == 8 and ng % 2 == 0 and own % 2 == 0 and tx % qy == 0 and tx >= HMAX and tx % 2 == 0
    f32 = jnp.float32
    dma = pltpu.SemaphoreType.DMA
    vmem = pl.BlockSpec(memory_space=pltpu.VMEM)
    gathered = pl.pallas_call(
        functools.partial(kernel, sizes),
        out_shape=jax.ShapeDtypeStruct((ng, own // 2, tx, sub, nz), f32),
        in_specs=[vmem] * 6 + [pl.BlockSpec(memory_space=pltpu.SMEM)],
        out_specs=vmem,
        scratch_shapes=[
            pltpu.VMEM((2, 2, 2, tx, sub, nz), f32),
            pltpu.VMEM((tx, sub, nz), f32),
            pltpu.VMEM((tx, sub, nz), f32),
            pltpu.VMEM((tx, sub, nz), f32),
            pltpu.VMEM((tx, sub, nz), f32),
            pltpu.VMEM((2, tx * sub, nz), f32),
            pltpu.VMEM((2, tx * sub, shots * nrec), jnp.bfloat16),
            pltpu.VMEM((2, shots * nrec, nz), jnp.bfloat16),
            pltpu.VMEM((blocks, 2, tx + 2 * HMAX, sub, nz), f32),
            pltpu.VMEM((nh, tx, sub, nz), f32),
            pltpu.VMEM((ng, own // 2, tx, sub, nz), f32),
            pltpu.VMEM((2, 2, 2, sub, nz), f32),
            pltpu.VMEM((2, 2, 2, groups, sub, nz), f32),
            pltpu.VMEM((2, 2, 2, groups, sub, nz), f32),
            dma((2, 2, 4)),
            dma((2, 2, 4)),
            dma((blocks, 2, 2)),
            dma((blocks, 2, 2)),
            dma((ng,)),
            dma((ng,)),
        ],
        compiler_params=pltpu.CompilerParams(
            collective_id=0, has_side_effects=True, vmem_limit_bytes=56 * 1024 * 1024
        ),
    )(courant, epsilon, delta, checkpoint, positions.transpose(1, 0, 2), amplitudes, offsets)
    cut = math.gcd(tx, 4)
    span = tx // cut
    return pl.pallas_call(
        place,
        grid=(cut,),
        out_shape=jax.ShapeDtypeStruct((own, tx, ty, nz), f32),
        in_specs=[pl.BlockSpec((ng, own // 2, span, sub, nz), lambda n: (0, 0, n, 0, 0))],
        out_specs=pl.BlockSpec((own, span, ty, nz), lambda n: (0, n, 0, 0)),
    )(gathered)


def solution(mesh):
    sizes = tuple(mesh.shape[axis] for axis in ("grp", "gx", "gy"))
    return jax.shard_map(
        functools.partial(shards, sizes),
        mesh=mesh,
        in_specs=(
            P(None, None, None, "gx", "gy", None),
            P("gx", "gy", None),
            P("gx", "gy", None),
            P("gx", "gy", None),
            P(),
            P(),
            P(),
        ),
        out_specs=P("grp", "gx", "gy", None),
        check_vma=False,
    )
```

profile of v0, /device:TPU:24, one launch (start us, length us, event | category | flops | bytes accessed | tf_op | source)
XLA Modules:
  0.0 89.2 jit_solution(12828253141795375428)
XLA Ops:
  0.0 85.8 %shard_map.73.gathered = f32[4,2,16,8,256]{4,3,2,1,0:T(8,128)} custom-call(f32[16,16,256]{2,1,0:T(8,128)} %courant.1, f32[16,16,256]{2,1,0:T(8,128)} %epsilon.1, f32[16,16,256]{2,1,0:T(8,128)} %delta.1, f32[2,2,2,16,16,256]{5,4,3,2,1,0:T(8,128)} %checkpoint.1, s32[3,4,512]{2,1,0:T(4,128)} %bitcast.1, f32[4,16,512]{2,1,0:T(8,128)} %amplitudes.1, s32[16]{0:T(128)} %offsets.1), custom_call_target="tpu_custom_call" | custom-call | tf_op jit(solution)/shard_map/pallas_call | solution.py:374
  85.8 3.4 %shard_map.74 = f32[4,16,16,256]{3,2,1,0:T(8,128)} custom-call(f32[4,2,16,8,256]{4,3,2,1,0:T(8,128)} %shard_map.73.gathered), custom_call_target="tpu_custom_call" | custom-call | tf_op jit(solution)/shard_map/pallas_call | solution.py:407
where the time goes:
time: 89.4 us; the launch traced here: 89.2 us
  Pallas kernels  89.2 us (100%)
    pallas_call x1, Pallas kernels, shards(): pl.pallas_call(functools.partial(kernel, sizes), out_shape=jax.ShapeDtype...  85.8 us
    pallas_call x1, Pallas kernels, shards(): pl.pallas_call(place, grid=(cut,), out_shape=jax.ShapeDtypeStruct((own, t...  3.39 us

commit v1 on v0

v1 whole, which is shorter than its diff:
```python
import functools
import jax
import jax.numpy as jnp
from jax import lax
from jax.experimental import pallas as pl
from jax.experimental.pallas import tpu as pltpu
from jax.sharding import PartitionSpec as P

SNAP = 4
HMAX = 8
PAIR = 2
ROWS = 8
LANES = 128
MESH = pl.DeviceIdType.MESH


def kernel(sizes, courant, epsilon, delta, checkpoint, positions, amplitudes, offsets, out,
           sg, sh, raw, cg, ch, pickg, pickh, spot, injg, injh, injb, ix, iy, idg, py, rx, ry, rd,
           snaps, fringe, outgoing, inbox,
           ls, isx, irx, isy, iry, isd, ird, hsx, hrx, hsy, hry, hsd, hrd, xs, xr, gs, gr):
    ng, nx, ny = sizes
    tx, ty, nz = courant.shape
    nrec = positions.shape[2]
    steps = amplitudes.shape[1]
    nh = offsets.shape[0]
    own = nh // ng
    turns = steps // PAIR
    blocks = steps // SNAP
    per = SNAP // PAIR
    d, a, b = lax.axis_index("grp"), lax.axis_index("gx"), lax.axis_index("gy")
    half = d % 2
    pair = d - half
    partner = {"grp": pair + 1 - half, "gx": a, "gy": b}
    edge = 1 if nx == 2 else 2
    width = tx + edge
    lead = a if nx == 2 else 1
    start = PAIR - lead
    right = PAIR + tx
    f32 = jnp.float32

    xside = (a > 0, a < nx - 1)
    yside = (b > 0, b < ny - 1)
    xdev = tuple({"grp": d, "gx": a + 2 * i - 1, "gy": b} for i in range(2))
    ydev = tuple({"grp": d, "gx": a, "gy": b + 2 * i - 1} for i in range(2))
    corners = [(i, j) for i in range(2) for j in range(2)]
    cthere = {(i, j): xside[i] & yside[j] for i, j in corners}
    cdev = {(i, j): {"grp": d, "gx": a + 2 * i - 1, "gy": b + 2 * j - 1} for i, j in corners}

    barrier = pltpu.get_barrier_semaphore()
    met = [(xside[i], xdev[i]) for i in range(2)] + [(yside[i], ydev[i]) for i in range(2)]
    met += [(cthere[c], cdev[c]) for c in corners]
    pl.semaphore_signal(barrier, inc=1, device_id=partner, device_id_type=MESH)
    for there, device in met:
        @pl.when(there)
        def _(device=device):
            pl.semaphore_signal(barrier, inc=1, device_id=device, device_id_type=MESH)

    models = (courant, epsilon, delta)

    def model_load(n):
        return pltpu.make_async_copy(models[n], raw.at[n], ls.at[n])

    def state_load(moment, field):
        return pltpu.make_async_copy(
            checkpoint.at[half, moment, field], sg.at[0, moment, field, pl.ds(PAIR, tx)], ls.at[3 + 2 * moment + field]
        )

    for n in range(3):
        model_load(n).start()

    for moment in range(2):
        for field in range(2):
            state_load(moment, field).start()

    big = jnp.zeros((ty, nz), f32)
    zero = jnp.zeros((ROWS, nz), f32)
    row = lax.broadcasted_iota(jnp.int32, (ROWS, nz), 0)
    lane = lax.broadcasted_iota(jnp.int32, (ROWS, LANES), 1)
    top, bottom, upper = row == 0, row == ROWS - 1, row < ROWS // 2

    def turn(v, shift, axis=0):
        shift = shift % v.shape[axis]
        return v if shift == 0 else pltpu.roll(v, shift, axis)

    for moment in range(2):
        for field in range(2):
            for x in range(tx + 2 * PAIR):
                sg[1, moment, field, x] = big
                for r in range(2):
                    sh[r, moment, field, x] = zero
            for x in (0, 1, right, right + 1):
                sg[0, moment, field, x] = big
    for n in range(3):
        for x in (0, 1, right, right + 1):
            cg[n, x] = big
            ch[n, x] = zero
    for side in range(2):
        @pl.when(jnp.logical_not(yside[side]))
        def _(side=side):
            for x in range(tx):
                iy[side, x] = zero
                for slot in range(2):
                    for r in range(2):
                        ry[slot, r, side, x] = zero
    for i, j in corners:
        @pl.when(jnp.logical_not(cthere[i, j]))
        def _(i=i, j=j):
            idg[i, j] = zero
            for slot in range(2):
                for r in range(2):
                    rd[slot, r, i, j] = zero

    total = 1
    for there, _ in met:
        total = total + there.astype(jnp.int32)
    pl.semaphore_wait(barrier, total)

    def first_x(side, n, arrival=False):
        last = tx - 1 if side else 0
        if n == 0:
            rows, target = pl.ds(tx - PAIR if side else 0, PAIR), pl.ds(0, PAIR)
        else:
            rows, target = pl.ds(last, 1), pl.ds(n + 1, 1)
        if n < 4:
            source = checkpoint.at[half, n // 2, n % 2, rows]
        else:
            source = models[n - 4].at[rows]
        into = side if arrival else 1 - side
        target = ix.at[into, target]
        return pltpu.make_async_remote_copy(
            src_ref=target if arrival else source, dst_ref=target, send_sem=isx.at[side, n],
            recv_sem=irx.at[into, n], device_id=xdev[side], device_id_type=MESH,
        )

    for side in range(2):
        @pl.when(xside[side])
        def _(side=side):
            for n in range(7):
                first_x(side, n).start()

    for n in range(3):
        model_load(n).wait()

    for moment in range(2):
        for field in range(2):
            state_load(moment, field).wait()

    def ends(v):
        return v[:ROWS], v[ty - ROWS:]

    for x in range(tx):
        tiles = [ends(sg[0, n // 2, n % 2, PAIR + x]) for n in range(4)]
        tiles += [ends(raw[n, x]) for n in range(3)]
        lower, higher = tiles[0]
        for n in range(1, 7):
            lower = jnp.where(row == n + 1, turn(tiles[n][0], n + 1), lower)
            higher = jnp.where(row == ROWS - 2 - n, turn(tiles[n][1], -n - 1), higher)
        py[0, 0, x] = lower
        py[0, 1, x] = higher

    def y_copy(r, target, send, recv, side, arrival=False):
        into = side if arrival else 1 - side
        return pltpu.make_async_remote_copy(
            src_ref=target.at[into] if arrival else py.at[r, side], dst_ref=target.at[into], send_sem=send.at[side],
            recv_sem=recv.at[into], device_id=ydev[side], device_id_type=MESH,
        )

    def d_copy(r, target, send, recv, corner, arrival=False):
        i, j = corner
        u, v = corner if arrival else (1 - i, 1 - j)
        return pltpu.make_async_remote_copy(
            src_ref=target.at[u, v] if arrival else py.at[r, j, tx - 1 if i else 0], dst_ref=target.at[u, v],
            send_sem=send.at[i, j], recv_sem=recv.at[u, v], device_id=cdev[corner], device_id_type=MESH,
        )

    for c in corners:
        @pl.when(cthere[c])
        def _(c=c):
            d_copy(0, idg, isd, ird, c).start()
    for side in range(2):
        @pl.when(yside[side])
        def _(side=side):
            y_copy(0, iy, isy, iry, side).start()

    def mix(c, e, v):
        return c + 2.0 * c * e, c * jnp.sqrt(2.0 * v + 1.0), c

    for x in range(tx):
        parts = mix(raw[0, x], raw[1, x], raw[2, x])
        for n in range(3):
            cg[n, PAIR + x] = parts[n]

    count = lax.broadcasted_iota(jnp.int32, (ty, nrec), 0)
    level = lax.broadcasted_iota(jnp.int32, (nz, nrec), 0)
    for r in range(2):
        line = pl.ds(2 * half + r, 1)
        px = positions[0, line, :] - (a * tx - lead)
        qy = positions[1, line, :] - b * ty
        pz = positions[2, line, :]
        column = (px >= 0) & (px < width)
        cell = jnp.where(column & (qy >= 0) & (qy < ty), px * ty + qy, -1)
        brim = jnp.where(column & (qy == ty), px * ROWS, jnp.where(column & (qy == -1), px * ROWS + ROWS - 1, -1))
        for w in range(width):
            pickg[r, pl.ds(w * ty, ty), :] = jnp.where(count + w * ty == cell, 1.0, 0.0).astype(jnp.bfloat16)
        for w in range((width + 1) // 2):
            pickh[r, pl.ds(w * ty, ty), :] = jnp.where(count + w * ty == brim, 1.0, 0.0).astype(jnp.bfloat16)
        where_z = jnp.where(level == pz, 1.0, 0.0).T.astype(jnp.bfloat16)
        spot[r, pl.ds(0, nrec), :] = where_z
        spot[r, pl.ds(nrec, nrec), :] = where_z

    def blank(j, carry):
        for r in range(2):
            for x in range(HMAX):
                snaps[j, r, x] = big
                snaps[j, r, HMAX + tx + x] = big
        return carry

    lax.fori_loop(0, blocks, blank, 0)

    def inject(turn_index, r):
        def strength(moment):
            s = jnp.broadcast_to(amplitudes[2 * half + r, pl.ds(moment, 1), :], (ty, nrec))
            high = s.astype(jnp.bfloat16)
            low = (s - high.astype(f32)).astype(jnp.bfloat16)
            return high, low

        def weigh(ref, base, n, parts):
            p = ref[r, pl.ds(base + n * ty, ty), :]
            return jnp.concatenate([p * parts[0], p * parts[1]], axis=1)

        one, two = strength(PAIR * turn_index), strength(PAIR * turn_index + 1)
        ours = pl.multiple_of(lead * ty, ty) if nx == 2 else lead * ty
        rows = [weigh(pickg, 0, n, one) for n in range(width)]
        rows += [weigh(pickh, 0, n, one) for n in range((width + 1) // 2)]
        rows += [weigh(pickg, ours, n, two) for n in range(tx)]
        found = jnp.dot(jnp.concatenate(rows, axis=0), spot[r], preferred_element_type=f32)
        low, high = width * ty, (width + (width + 1) // 2) * ty
        injg[r] = found[:low]
        injh[r] = found[low:high]
        injb[r] = found[high:]

    def down(v):
        tiles = [v[:, n * LANES:(n + 1) * LANES] for n in range(nz // LANES)]
        fore = [turn(t, 1, 1) for t in tiles]
        back = [turn(t, -1, 1) for t in tiles]
        sums = []
        for n, t in enumerate(tiles):
            before = jnp.where(lane == 0, fore[n - 1] if n else 0.0, fore[n])
            after = jnp.where(lane == LANES - 1, back[n + 1] if n + 1 < len(tiles) else 0.0, back[n])
            sums.append(before + after - 2.0 * t)
        return jnp.concatenate(sums, axis=1)

    def tiles_of(r, now, field, slot, brim):
        v = sg[r, now, field, slot]
        parts = [v[n * ROWS:(n + 1) * ROWS] for n in range(ty // ROWS)]
        return parts + ([sh[r, now, field, slot]] if brim else [])

    def advance(r, now, base, span, brim, gref, href):
        then = 1 - now
        full = ty // ROWS
        size = full + (1 if brim else 0)
        behind, here = tiles_of(r, now, 0, base - 1, brim), tiles_of(r, now, 0, base, True)
        for w in range(span):
            slot = base + w
            ahead = tiles_of(r, now, 0, slot + 1, True)
            ups, downs = [turn(t, 1) for t in here], [turn(t, -1) for t in here]
            for n in range(size):
                north = jnp.where(top, ups[n - 1], ups[n])
                south = jnp.where(bottom, downs[(n + 1) % (full + 1)], downs[n])
                m = here[n]
                across = (north + south) + (behind[n] + ahead[n]) - 4.0 * m
                if n < full:
                    part = pl.ds(n * ROWS, ROWS)
                    cur = sg.at[r, now, 1, slot, part]
                    prev = (sg.at[r, then, 0, slot, part], sg.at[r, then, 1, slot, part])
                    hor, cpl, ver = (cg[k, slot, part] for k in range(3))
                    source = gref[r, pl.ds(w * ty + n * ROWS, ROWS), :]
                else:
                    cur, prev = sh.at[r, now, 1, slot], (sh.at[r, then, 0, slot], sh.at[r, then, 1, slot])
                    hor, cpl, ver = (ch[k, slot] for k in range(3))
                    source = href[r, pl.ds(w * ROWS, ROWS), :]
                aux = cur[...]
                vertical = down(aux)
                prev[0][...] = 2.0 * m - prev[0][...] + hor * across + cpl * vertical + source
                prev[1][...] = 2.0 * aux - prev[1][...] + cpl * across + ver * vertical + source
            behind, here = here, ahead

    def first_merge():
        for side in range(2):
            @pl.when(yside[side])
            def _(side=side):
                y_copy(0, iy, isy, iry, side, True).wait_recv()
                y_copy(0, iy, isy, iry, side).wait_send()
        for c in corners:
            @pl.when(cthere[c])
            def _(c=c):
                d_copy(0, idg, isd, ird, c, True).wait_recv()
                d_copy(0, idg, isd, ird, c).wait_send()
        for side in range(2):
            @pl.when(xside[side])
            def _(side=side):
                for n in range(7):
                    first_x(side, n, True).wait_recv()
                    first_x(side, n).wait_send()

        for x in range(tx):
            below, above = iy[0, x], iy[1, x]

            def field(n):
                if n == 0:
                    return jnp.where(upper, above, below)
                return jnp.where(upper, turn(above, -n - 1), turn(below, n + 1))

            for n in range(4):
                sh[0, n // 2, n % 2, PAIR + x] = field(n)
            parts = mix(*(jnp.where(top | bottom, field(4 + n), 0.0) for n in range(3)))
            for n in range(3):
                ch[n, PAIR + x] = parts[n]
        for side in range(2):
            @pl.when(xside[side])
            def _(side=side):
                near, low = (right, right) if side else (1, 0)
                for n in range(PAIR):
                    sg[0, 0, 0, low + n] = ix[side, n]
                for n in range(1, 4):
                    sg[0, n // 2, n % 2, near] = ix[side, n + 1]
                parts = mix(ix[side, 5], ix[side, 6], ix[side, 7])
                for n in range(3):
                    cg[n, near] = parts[n]
                sh[0, 0, 0, near] = jnp.where(upper, idg[side, 1], idg[side, 0])

    def x_copy(slot, r, side, n, arrival=False):
        if n == 0:
            rows, target = pl.ds(right - PAIR if side else PAIR, PAIR), pl.ds(0, PAIR)
        else:
            rows, target = pl.ds(right - 1 if side else PAIR, 1), pl.ds(PAIR, 1)
        into = side if arrival else 1 - side
        target = rx.at[slot, r, into, target]
        return pltpu.make_async_remote_copy(
            src_ref=target if arrival else sg.at[r, 0, n, rows], dst_ref=target, send_sem=hsx.at[slot, r, side, n],
            recv_sem=hrx.at[slot, r, into, n], device_id=xdev[side], device_id_type=MESH,
        )

    def halo_y(slot, r, side, arrival=False):
        return y_copy(r, ry.at[slot, r], hsy.at[slot, r], hry.at[slot, r], side, arrival)

    def halo_d(slot, r, corner, arrival=False):
        return d_copy(r, rd.at[slot, r], hsd.at[slot, r], hrd.at[slot, r], corner, arrival)

    def merge(slot, r):
        for side in range(2):
            @pl.when(yside[side])
            def _(side=side):
                halo_y(slot, r, side, True).wait_recv()
                halo_y(slot, r, side).wait_send()
        for x in range(tx):
            below, above = ry[slot, r, 0, x], ry[slot, r, 1, x]
            sh[r, 0, 0, PAIR + x] = jnp.where(upper, above, below)
            sh[r, 0, 1, PAIR + x] = jnp.where(upper, turn(above, -2), turn(below, 2))
        for c in corners:
            @pl.when(cthere[c])
            def _(c=c):
                halo_d(slot, r, c, True).wait_recv()
                halo_d(slot, r, c).wait_send()
        for side in range(2):
            @pl.when(xside[side])
            def _(side=side):
                for n in range(2):
                    x_copy(slot, r, side, n, True).wait_recv()
                    x_copy(slot, r, side, n).wait_send()
                near, low = (right, right) if side else (1, 0)
                for n in range(PAIR):
                    sg[r, 0, 0, low + n] = rx[slot, r, side, n]
                sg[r, 0, 1, near] = rx[slot, r, side, PAIR]
                sh[r, 0, 0, near] = jnp.where(upper, rd[slot, r, side, 1], rd[slot, r, side, 0])

    def send(slot, r):
        for side in range(2):
            @pl.when(xside[side])
            def _(side=side):
                for n in range(2):
                    x_copy(slot, r, side, n).start()
        for x in range(tx):
            m, w = ends(sg[r, 0, 0, PAIR + x]), ends(sg[r, 0, 1, PAIR + x])
            py[r, 0, x] = jnp.where(row == 2, turn(w[0], 2), m[0])
            py[r, 1, x] = jnp.where(row == ROWS - 3, turn(w[1], -2), m[1])
        for c in corners:
            @pl.when(cthere[c])
            def _(c=c):
                halo_d(slot, r, c).start()
        for side in range(2):
            @pl.when(yside[side])
            def _(side=side):
                halo_y(slot, r, side).start()

    def fringe_copy(j, r, side, arrival=False):
        into = side if arrival else 1 - side
        source = snaps.at[j, r, pl.ds(tx, HMAX) if side else pl.ds(HMAX, HMAX)]
        target = fringe.at[j, r, into]
        return pltpu.make_async_remote_copy(
            src_ref=target if arrival else source, dst_ref=target, send_sem=xs.at[j, r, side],
            recv_sem=xr.at[j, r, into], device_id=xdev[side], device_id_type=MESH,
        )

    def send_fringe(j, r):
        for side in range(2):
            @pl.when(xside[side])
            def _(side=side):
                fringe_copy(j, r, side).start()

    def merge_fringe(j, r):
        for side in range(2):
            @pl.when(xside[side])
            def _(side=side):
                fringe_copy(j, r, side, True).wait_recv()
                fringe_copy(j, r, side).wait_send()
                for x in range(HMAX):
                    snaps[j, r, side * (HMAX + tx) + x] = fringe[j, r, side, x]

    def cycle(e, carry):
        for r in range(2):
            inject(e, r)

        @pl.when(e == 0)
        def _():
            first_merge()

        for r in range(2):
            @pl.when(e > 0)
            def _(r=r):
                merge(e % 2, r)

            advance(r, 0, start, width, True, injg, injh)
            advance(r, 1, PAIR, tx, False, injb, None)

            @pl.when(e < turns - 1)
            def _(r=r):
                send((e + 1) % 2, r)

        @pl.when(e % per == per - 1)
        def _():
            j = e // per
            for r in range(2):
                for x in range(tx):
                    snaps[j, r, HMAX + x] = sg[r, 0, 0, PAIR + x]
            send_fringe(j, 0)

        @pl.when(e == turns - 1)
        def _():
            send_fringe(blocks - 1, 1)

        @pl.when((e % per == 0) & (e > 0))
        def _():
            send_fringe(e // per - 1, 1)

        return carry

    lax.fori_loop(0, turns, cycle, 0)

    def swap_copy(n, rows, part):
        return pltpu.make_async_remote_copy(
            src_ref=outgoing.at[n, rows], dst_ref=inbox.at[n, rows], send_sem=gs.at[part, n], recv_sem=gr.at[part, n],
            device_id=partner, device_id_type=MESH,
        )

    def product(shift, x):
        sums = None
        for j in range(blocks):
            term = snaps[j, 0, HMAX - shift + x] * snaps[j, 1, HMAX + shift + x]
            sums = term if sums is None else sums + term
        return sums

    mid = tx // 2
    spans = [pl.ds(a * mid, mid), pl.ds((1 - a) * mid, mid)] if nx == 2 else [pl.ds(0, mid), pl.ds(mid, mid)]

    def fringes():
        for r in range(2):
            def one(j, carry, r=r):
                merge_fringe(j, r)
                return carry

            lax.fori_loop(0, blocks, one, 0)

    if nx != 2:
        fringes()
    for part, rows in enumerate(spans):
        if nx == 2 and part == 1:
            fringes()

        def theirs(n, carry, part=part, rows=rows):
            shift = offsets[pair * own + (1 - half) * own + n]
            for x in range(mid):
                outgoing[n, rows.start + x] = product(shift, rows.start + x)
            swap_copy(n, rows, part).start()
            return carry

        def ours(n, carry, rows=rows):
            shift = offsets[pair * own + half * own + n]
            for x in range(mid):
                out[n, rows.start + x] = product(shift, rows.start + x)
            return carry

        lax.fori_loop(0, own, theirs, 0)
        lax.fori_loop(0, own, ours, 0)
    for part, rows in enumerate(spans):
        def done(n, carry, part=part, rows=rows):
            swap_copy(n, rows, part).wait_recv()
            swap_copy(n, rows, part).wait_send()
            for x in range(mid):
                out[n, rows.start + x] = out[n, rows.start + x] + inbox[n, rows.start + x]
            return carry

        lax.fori_loop(0, own, done, 0)


def shards(sizes, checkpoint, courant, epsilon, delta, positions, amplitudes, offsets):
    ng, nx, ny = sizes
    shots = checkpoint.shape[0]
    tx, ty, nz = courant.shape
    nrec = positions.shape[2]
    steps = amplitudes.shape[1]
    blocks = steps // SNAP
    nh = offsets.shape[0]
    own = nh // ng
    assert ng == 2 * shots == 4 and ty == 2 * ROWS and tx >= HMAX and nz % LANES == 0 and nh % ng == 0 and nx > 1
    width = tx + (1 if nx == 2 else 2)
    wide = (width + 1) // 2
    slots = tx + 2 * PAIR
    f32, bf16 = jnp.float32, jnp.bfloat16
    dma = pltpu.SemaphoreType.DMA
    vmem = pl.BlockSpec(memory_space=pltpu.VMEM)
    anywhere = pl.BlockSpec(memory_space=pl.ANY)
    return pl.pallas_call(
        functools.partial(kernel, sizes),
        out_shape=jax.ShapeDtypeStruct((own, tx, ty, nz), f32),
        in_specs=[anywhere] * 4 + [vmem] * 2 + [pl.BlockSpec(memory_space=pltpu.SMEM)],
        out_specs=vmem,
        scratch_shapes=[
            pltpu.VMEM((2, 2, 2, slots, ty, nz), f32),
            pltpu.VMEM((2, 2, 2, slots, ROWS, nz), f32),
            pltpu.VMEM((3, tx, ty, nz), f32),
            pltpu.VMEM((3, slots, ty, nz), f32),
            pltpu.VMEM((3, slots, ROWS, nz), f32),
            pltpu.VMEM((2, width * ty, nrec), bf16),
            pltpu.VMEM((2, wide * ty, nrec), bf16),
            pltpu.VMEM((2, 2 * nrec, nz), bf16),
            pltpu.VMEM((2, width * ty, nz), f32),
            pltpu.VMEM((2, wide * ty, nz), f32),
            pltpu.VMEM((2, tx * ty, nz), f32),
            pltpu.VMEM((2, 8, ty, nz), f32),
            pltpu.VMEM((2, tx, ROWS, nz), f32),
            pltpu.VMEM((2, 2, ROWS, nz), f32),
            pltpu.VMEM((2, 2, tx, ROWS, nz), f32),
            pltpu.VMEM((2, 2, 2, PAIR + 1, ty, nz), f32),
            pltpu.VMEM((2, 2, 2, tx, ROWS, nz), f32),
            pltpu.VMEM((2, 2, 2, 2, ROWS, nz), f32),
            pltpu.VMEM((blocks, 2, tx + 2 * HMAX, ty, nz), f32),
            pltpu.VMEM((blocks, 2, 2, HMAX, ty, nz), f32),
            pltpu.VMEM((own, tx, ty, nz), f32),
            pltpu.VMEM((own, tx, ty, nz), f32),
            dma((7,)),
            dma((2, 7)),
            dma((2, 7)),
            dma((2,)),
            dma((2,)),
            dma((2, 2)),
            dma((2, 2)),
            dma((2, 2, 2, 2)),
            dma((2, 2, 2, 2)),
            dma((2, 2, 2)),
            dma((2, 2, 2)),
            dma((2, 2, 2, 2)),
            dma((2, 2, 2, 2)),
            dma((blocks, 2, 2)),
            dma((blocks, 2, 2)),
            dma((2, own)),
            dma((2, own)),
        ],
        compiler_params=pltpu.CompilerParams(
            collective_id=0, has_side_effects=True, vmem_limit_bytes=32 * 1024 * 1024
        ),
    )(courant, epsilon, delta, checkpoint, positions.transpose(1, 0, 2), amplitudes, offsets)


def solution(mesh):
    sizes = tuple(mesh.shape[axis] for axis in ("grp", "gx", "gy"))
    return jax.shard_map(
        functools.partial(shards, sizes),
        mesh=mesh,
        in_specs=(
            P(None, None, None, "gx", "gy", None),
            P("gx", "gy", None),
            P("gx", "gy", None),
            P("gx", "gy", None),
            P(),
            P(),
            P(),
        ),
        out_specs=P("grp", "gx", "gy", None),
        check_vma=False,
    )
```

time: 89.4 us -> 81.8 us (0.915)
  the two profiles are of different devices: /device:TPU:24 before, /device:TPU:0 now
where the time goes in v1:
time: 81.8 us; the launch traced here: 81.5 us
  Pallas kernels  73.8 us (90%)
  local copies, waits for them, and re-layouts  7.71 us (9%)
    pallas_call x1, Pallas kernels, shards(): pl.pallas_call(functools.partial(kernel, sizes), out_shape=jax.ShapeDtype...  73.8 us
    unnamed x15, local copies, waits for them, and re-layouts  7.71 us

profile of v1, /device:TPU:0, one launch (start us, length us, event | category | flops | bytes accessed | tf_op | source)
XLA Modules:
  0.0 81.5 jit_solution(17238115716800320040)
XLA Ops:
  0.0 0.0 copy-start
  0.0 1.6 %copy-done = f32[2,2,2,16,16,256]{5,4,3,2,1,0:T(8,128)S(1)} copy-done((f32[2,2,2,16,16,256]{5,4,3,2,1,0:T(8,128)S(1)}, f32[2,2,2,16,16,256]{5,4,3,2,1,0:T(8,128)}, u32[]{:S(2)}) %copy-start) | copy-done | bytes 2097176
  1.6 0.0 copy-start.1
  1.6 0.9 %copy-done.1 = f32[16,16,256]{2,1,0:T(8,128)S(1)} copy-done((f32[16,16,256]{2,1,0:T(8,128)S(1)}, f32[16,16,256]{2,1,0:T(8,128)}, u32[]{:S(2)}) %copy-start.1) | copy-done | bytes 262168
  2.5 0.0 copy-start.2
  2.5 0.9 %copy-done.2 = f32[16,16,256]{2,1,0:T(8,128)S(1)} copy-done((f32[16,16,256]{2,1,0:T(8,128)S(1)}, f32[16,16,256]{2,1,0:T(8,128)}, u32[]{:S(2)}) %copy-start.2) | copy-done | bytes 262168
  3.5 0.0 copy-start.3
  3.5 0.9 %copy-done.3 = f32[16,16,256]{2,1,0:T(8,128)S(1)} copy-done((f32[16,16,256]{2,1,0:T(8,128)S(1)}, f32[16,16,256]{2,1,0:T(8,128)}, u32[]{:S(2)}) %copy-start.3) | copy-done | bytes 262168
  4.4 0.0 copy-start.4
  4.4 0.9 %copy-done.4 = f32[4,16,512]{2,1,0:T(8,128)S(1)} copy-done((f32[4,16,512]{2,1,0:T(8,128)S(1)}, f32[4,16,512]{2,1,0:T(8,128)}, u32[]{:S(2)}) %copy-start.4) | copy-done | bytes 131096
  5.3 0.0 copy-start.5
  5.4 0.7 copy-done.5
  6.1 0.0 copy-start.6
  6.1 0.7 copy-done.6
  6.7 73.8 %shard_map.73 = f32[4,16,16,256]{3,2,1,0:T(8,128)S(1)} custom-call(f32[16,16,256]{2,1,0:T(8,128)S(1)} %copy-done.1, f32[16,16,256]{2,1,0:T(8,128)S(1)} %copy-done.2, f32[16,16,256]{2,1,0:T(8,128)S(1)} %copy-done.3, f32[2,2,2,16,16,256]{5,4,3,2,1,0:T(8,128)S(1)} %copy-done, s32[3,4,512]{2,1,0:T(4,128)S(1)} %bitcast.1, f32[4,16,512]{2,1,0:T(8,128)S(1)} %copy-done.4, ...), custom_call_target="tpu_custom_call" | custom-call | tf_op jit(solution)/shard_map/pallas_call | solution.py:533
  80.5 1.0 %copy.9 = f32[4,16,16,256]{3,2,1,0:T(8,128)} copy(f32[4,16,16,256]{3,2,1,0:T(8,128)S(1)} %shard_map.73) | data formatting | bytes 2097152
Async XLA Ops:
  0.0 1.6 %copy-start = (f32[2,2,2,16,16,256]{5,4,3,2,1,0:T(8,128)S(1)}, f32[2,2,2,16,16,256]{5,4,3,2,1,0:T(8,128)}, u32[]{:S(2)}) copy-start(f32[2,2,2,16,16,256]{5,4,3,2,1,0:T(8,128)} %checkpoint.1) | copy-start | bytes 6291460
  1.6 0.9 %copy-start.1 = (f32[16,16,256]{2,1,0:T(8,128)S(1)}, f32[16,16,256]{2,1,0:T(8,128)}, u32[]{:S(2)}) copy-start(f32[16,16,256]{2,1,0:T(8,128)} %courant.1) | copy-start | bytes 786436
  2.5 0.9 %copy-start.2 = (f32[16,16,256]{2,1,0:T(8,128)S(1)}, f32[16,16,256]{2,1,0:T(8,128)}, u32[]{:S(2)}) copy-start(f32[16,16,256]{2,1,0:T(8,128)} %epsilon.1) | copy-start | bytes 786436
  3.5 0.9 %copy-start.3 = (f32[16,16,256]{2,1,0:T(8,128)S(1)}, f32[16,16,256]{2,1,0:T(8,128)}, u32[]{:S(2)}) copy-start(f32[16,16,256]{2,1,0:T(8,128)} %delta.1) | copy-start | bytes 786436
  4.4 0.9 %copy-start.4 = (f32[4,16,512]{2,1,0:T(8,128)S(1)}, f32[4,16,512]{2,1,0:T(8,128)}, u32[]{:S(2)}) copy-start(f32[4,16,512]{2,1,0:T(8,128)} %amplitudes.1) | copy-start | bytes 393220
  5.3 0.7 copy-start.5
  6.1 0.7 copy-start.6

commit v2 on v1

--- a/solution.py
+++ b/solution.py
@@ -577,7 +577,7 @@
             dma((2, own)),
         ],
         compiler_params=pltpu.CompilerParams(
-            collective_id=0, has_side_effects=True, vmem_limit_bytes=32 * 1024 * 1024
+            collective_id=0, has_side_effects=True, vmem_limit_bytes=58720256
         ),
     )(courant, epsilon, delta, checkpoint, positions.transpose(1, 0, 2), amplitudes, offsets)
 

time: 81.8 us -> 77.8 us (0.951)
  local copies, waits for them, and re-layouts: 7.71 us -> 2.26 us
  Pallas kernels: 73.8 us -> 75.3 us
    unnamed x15 -> x1, local copies, waits for them, and re-layouts: 7.71 us -> 2.26 us
    pallas_call x1, Pallas kernels: 73.8 us -> 75.3 us  [shards(): pl.pallas_call(functools.partial(kernel, sizes), out_shape=jax.ShapeDtype...]
where the time goes in v2:
time: 77.8 us; the launch traced here: 77.6 us
  Pallas kernels  75.3 us (97%)
  local copies, waits for them, and re-layouts  2.26 us (3%)
    pallas_call x1, Pallas kernels, shards(): pl.pallas_call(functools.partial(kernel, sizes), out_shape=jax.ShapeDtype...  75.3 us
    unnamed x1, local copies, waits for them, and re-layouts  2.26 us

profile of v2, /device:TPU:0, one launch (start us, length us, event | category | flops | bytes accessed | tf_op | source)
XLA Modules:
  0.0 77.6 jit_solution(5566024609871051749)
XLA Ops:
  0.0 75.3 %shard_map.73 = f32[4,16,16,256]{3,2,1,0:T(8,128)} custom-call(f32[16,16,256]{2,1,0:T(8,128)} %courant.1, f32[16,16,256]{2,1,0:T(8,128)} %epsilon.1, f32[16,16,256]{2,1,0:T(8,128)} %delta.1, f32[2,2,2,16,16,256]{5,4,3,2,1,0:T(8,128)} %checkpoint.1, s32[3,4,512]{2,1,0:T(4,128)} %bitcast.1, f32[4,16,512]{2,1,0:T(8,128)} %amplitudes.1, s32[16]{0:T(128)} %offsets.1), custom_call_target="tpu_custom_call" | custom-call | tf_op jit(solution)/shard_map/pallas_call | solution.py:533
  75.4 2.3 %copy.9 = f32[4,16,16,256]{3,2,1,0:T(8,128)} copy(f32[4,16,16,256]{3,2,1,0:T(8,128)} %shard_map.73) | data formatting | bytes 2097152

commit v3 on v2

v3 whole, which is shorter than its diff:
```python
import functools
import jax
import jax.numpy as jnp
from jax import lax
from jax.experimental import pallas as pl
from jax.experimental.pallas import tpu as pltpu
from jax.sharding import PartitionSpec as P

SNAP = 4
HMAX = 8
PAIR = 2
ROWS = 8
LANES = 128
MESH = pl.DeviceIdType.MESH


def kernel(sizes, courant, epsilon, delta, checkpoint, positions, amplitudes, offsets, out,
           sg, sh, raw, cg, ch, pickg, pickh, pickb, spot, injg, injh, injb, ix, ixc, iy, idg, pi, py, pc, rx, ry, rd,
           snaps, fringe, outgoing,
           ls, isx, irx, isy, iry, isd, ird, hsx, hrx, hsy, hry, hsd, hrd, xs, xr, gs, gr):
    ng, nx, ny = sizes
    shots = checkpoint.shape[0]
    waves = 2 * shots
    tx, ty, nz = courant.shape
    nrec = positions.shape[2]
    steps = amplitudes.shape[1]
    own = offsets.shape[0] // ng
    turns = steps // PAIR
    blocks = steps // SNAP
    per = SNAP // PAIR
    d, a, b = lax.axis_index("grp"), lax.axis_index("gx"), lax.axis_index("gy")
    half = d % 2
    pair = d - half
    other = pair + 1 - half
    flip = b % 2
    hp = half + flip - 2 * half * flip
    partner = {"grp": other, "gx": a, "gy": b}
    width = tx + (1 if nx == 2 else 2)
    lead = a if nx == 2 else 1
    start = PAIR - lead
    right = PAIR + tx
    f32, bf16 = jnp.float32, jnp.bfloat16
    mine = pl.ds(pl.multiple_of(hp * ROWS, ROWS), ROWS)

    inner = (hp, 1 - hp)
    xside = (a > 0, a < nx - 1)
    yside = ((hp == 1) | (b > 0), (hp == 0) | (b < ny - 1))
    near_y = tuple((d + inner[i] * (other - d), b + (2 * i - 1) * (1 - inner[i])) for i in range(2))
    xdev = tuple({"grp": d, "gx": a + 2 * i - 1, "gy": b} for i in range(2))
    ydev = tuple({"grp": near_y[i][0], "gx": a, "gy": near_y[i][1]} for i in range(2))
    corners = [(i, j) for i in range(2) for j in range(2)]
    cthere = {(i, j): xside[i] & yside[j] for i, j in corners}
    cdev = {(i, j): {"grp": near_y[j][0], "gx": a + 2 * i - 1, "gy": near_y[j][1]} for i, j in corners}

    barrier = pltpu.get_barrier_semaphore()
    met = [(xside[i], xdev[i]) for i in range(2)] + [(yside[i], ydev[i]) for i in range(2)]
    met += [(cthere[c], cdev[c]) for c in corners]
    pl.semaphore_signal(barrier, inc=1, device_id=partner, device_id_type=MESH)
    for there, device in met:
        @pl.when(there)
        def _(device=device):
            pl.semaphore_signal(barrier, inc=1, device_id=device, device_id_type=MESH)

    models = (courant, epsilon, delta)

    def model_load(n):
        return pltpu.make_async_copy(models[n].at[:, mine, :], raw.at[n], ls.at[n])

    def state_load(s, moment, field):
        return pltpu.make_async_copy(
            checkpoint.at[s, moment, field, :, mine, :], sg.at[2 * s, moment, field, pl.ds(PAIR, tx)],
            ls.at[3 + 4 * s + 2 * moment + field],
        )

    loads = [(s, moment, field) for s in range(shots) for moment in range(2) for field in range(2)]
    for n in range(3):
        model_load(n).start()
    for load in loads:
        state_load(*load).start()

    zero = jnp.zeros((ROWS, nz), f32)
    row = lax.broadcasted_iota(jnp.int32, (ROWS, nz), 0)
    lane = lax.broadcasted_iota(jnp.int32, (ROWS, LANES), 1)
    top, bottom, upper = row == 0, row == ROWS - 1, row < ROWS // 2

    def turn(v, shift, axis=0):
        shift = shift % v.shape[axis]
        return v if shift == 0 else pltpu.roll(v, shift, axis)

    outer = (0, 1, right, right + 1)
    quad, mains = ROWS // PAIR, tx * PAIR // ROWS
    packs = mains + tx // ROWS

    def wipe(x, carry):
        for r in range(waves):
            for moment in range(2):
                for field in range(2):
                    if r % 2:
                        sg[r, moment, field, x] = zero
                    sh[r, moment, field, x] = zero
        return carry

    lax.fori_loop(0, tx + 2 * PAIR, wipe, 0)
    for x in outer:
        for s in range(shots):
            for moment in range(2):
                for field in range(2):
                    sg[2 * s, moment, field, x] = zero
        for n in range(3):
            cg[n, x] = zero
            ch[n, x] = zero
    for side in range(2):
        @pl.when(jnp.logical_not(yside[side]))
        def _(side=side):
            for x in range(tx):
                for s in range(shots):
                    iy[s, side, x] = zero
            for n in range(packs):
                for slot in range(2):
                    for r in range(waves):
                        ry[slot, r, side, n] = zero
    for i, j in corners:
        @pl.when(jnp.logical_not(cthere[i, j]))
        def _(i=i, j=j):
            for s in range(shots):
                idg[s, i, j] = zero
            for slot in range(2):
                for r in range(waves):
                    rd[slot, r, i, j] = zero[:1]

    total = 1
    for there, _ in met:
        total = total + there.astype(jnp.int32)
    pl.semaphore_wait(barrier, total)

    def first_x(side, s, n, arrival=False):
        last = pl.ds(tx - 1 if side else 0, 1)
        into = side if arrival else 1 - side
        if s < shots:
            rows = pl.ds(tx - PAIR if side else 0, PAIR) if n == 0 else last
            source = checkpoint.at[s, n // 2, n % 2, rows, mine, :]
            target = ix.at[into, s, pl.ds(0, PAIR) if n == 0 else pl.ds(n + 1, 1)]
        else:
            source, target = models[n].at[last, mine, :], ixc.at[into, pl.ds(n, 1)]
        return pltpu.make_async_remote_copy(
            src_ref=target if arrival else source, dst_ref=target, send_sem=isx.at[side, s, n],
            recv_sem=irx.at[into, s, n], device_id=xdev[side], device_id_type=MESH,
        )

    firsts = [(shots, n) for n in range(3)] + [(s, n) for s in range(shots) for n in range(4)]
    for side in range(2):
        @pl.when(xside[side])
        def _(side=side):
            for s, n in firsts:
                first_x(side, s, n).start()

    for n in range(3):
        model_load(n).wait()
    for load in loads:
        state_load(*load).wait()

    def first_y(s, side, arrival=False):
        into = side if arrival else 1 - side
        return pltpu.make_async_remote_copy(
            src_ref=iy.at[s, into] if arrival else pi.at[s, side], dst_ref=iy.at[s, into], send_sem=isy.at[s, side],
            recv_sem=iry.at[s, into], device_id=ydev[side], device_id_type=MESH,
        )

    def first_d(s, corner, arrival=False):
        i, j = corner
        u, v = corner if arrival else (1 - i, 1 - j)
        return pltpu.make_async_remote_copy(
            src_ref=idg.at[s, u, v] if arrival else pi.at[s, j, tx - 1 if i else 0], dst_ref=idg.at[s, u, v],
            send_sem=isd.at[s, i, j], recv_sem=ird.at[s, u, v], device_id=cdev[corner], device_id_type=MESH,
        )

    for s in range(shots):
        for x in range(tx):
            tiles = [sg[2 * s, n // 2, n % 2, PAIR + x] for n in range(4)]
            tiles += [raw[n, x] for n in range(3)] if s == 0 else []
            lower = higher = tiles[0]
            for n in range(1, len(tiles)):
                lower = jnp.where(row == n + 1, turn(tiles[n], n + 1), lower)
                higher = jnp.where(row == ROWS - 2 - n, turn(tiles[n], -n - 1), higher)
            pi[s, 0, x] = lower
            pi[s, 1, x] = higher
        for c in corners:
            @pl.when(cthere[c])
            def _(c=c, s=s):
                first_d(s, c).start()
        for side in range(2):
            @pl.when(yside[side])
            def _(side=side, s=s):
                first_y(s, side).start()

    def mix(c, e, v):
        return c + 2.0 * c * e, c * jnp.sqrt(2.0 * v + 1.0), c

    for x in range(tx):
        parts = mix(raw[0, x], raw[1, x], raw[2, x])
        for n in range(3):
            cg[n, PAIR + x] = parts[n]

    tile = 2 * ROWS
    wide = (width * ROWS + tile - 1) // tile
    count = lax.broadcasted_iota(jnp.int32, (tile, nrec), 0)
    level = lax.broadcasted_iota(jnp.int32, (nz, nrec), 0)
    for r in range(waves):
        px = positions[0, r:r + 1, :] - (a * tx - lead)
        qy = positions[1, r:r + 1, :] - (b * ty + hp * ROWS)
        pz = positions[2, r:r + 1, :]
        column = (px >= 0) & (px < width)
        within = (qy >= 0) & (qy < ROWS)
        cell = jnp.where(column & within, px * ROWS + qy, -1)
        brim = jnp.where(column & (qy == ROWS), px * ROWS, jnp.where(column & (qy == -1), px * ROWS + ROWS - 1, -1))
        core = jnp.where((px >= lead) & (px < lead + tx) & within, (px - lead) * ROWS + qy, -1)
        for ref, where, parts in ((pickg, cell, wide), (pickh, brim, wide), (pickb, core, tx * ROWS // tile)):
            for n in range(parts):
                ref[r, pl.ds(n * tile, tile), :] = jnp.where(count + n * tile == where, 1.0, 0.0).astype(bf16)
        where_z = jnp.where(level == pz, 1.0, 0.0).T.astype(bf16)
        spot[r, pl.ds(0, nrec), :] = where_z
        spot[r, pl.ds(nrec, nrec), :] = where_z

    def blank(j, carry):
        for r in range(waves):
            for x in range(HMAX):
                snaps[j, r, x] = zero
                snaps[j, r, HMAX + tx + x] = zero
        return carry

    lax.fori_loop(0, blocks, blank, 0)

    def inject(turn_index, r):
        def strength(moment):
            s = jnp.broadcast_to(amplitudes[r, pl.ds(moment, 1), :], (tile, nrec))
            high = s.astype(bf16)
            low = (s - high.astype(f32)).astype(bf16)
            return high, low

        def weigh(ref, n, parts):
            p = ref[r, pl.ds(n * tile, tile), :]
            return jnp.concatenate([p * parts[0], p * parts[1]], axis=1)

        one, two = strength(PAIR * turn_index), strength(PAIR * turn_index + 1)
        rows = [weigh(pickg, n, one) for n in range(wide)] + [weigh(pickh, n, one) for n in range(wide)]
        rows += [weigh(pickb, n, two) for n in range(tx * ROWS // tile)]
        found = jnp.dot(jnp.concatenate(rows, axis=0), spot[r], preferred_element_type=f32)
        injg[r] = found[:wide * tile]
        injh[r] = found[wide * tile:2 * wide * tile]
        injb[r] = found[2 * wide * tile:]

    def down(v):
        tiles = [v[:, n * LANES:(n + 1) * LANES] for n in range(nz // LANES)]
        fore = [turn(t, 1, 1) for t in tiles]
        back = [turn(t, -1, 1) for t in tiles]
        sums = []
        for n, t in enumerate(tiles):
            before = jnp.where(lane == 0, fore[n - 1] if n else 0.0, fore[n])
            after = jnp.where(lane == LANES - 1, back[n + 1] if n + 1 < len(tiles) else 0.0, back[n])
            sums.append(before + after - 2.0 * t)
        return jnp.concatenate(sums, axis=1)

    def advance(r, now, base, order, brim, gref, href):
        then = 1 - now

        def row_of(w, deep=True):
            slot = base + w
            return [sg[r, now, 0, slot]] + ([sh[r, now, 0, slot]] if deep else [])

        last = None
        for w in order:
            slot = base + w
            if last is not None and w == last + 1:
                behind, here = here, ahead
            else:
                behind, here = row_of(w - 1, brim), row_of(w)
            ahead = row_of(w + 1)
            last = w
            ups, downs = [turn(t, 1) for t in here], [turn(t, -1) for t in here]
            for n in range(2 if brim else 1):
                grid, coefs, source = (sh, ch, href) if n else (sg, cg, gref)
                north = jnp.where(top, ups[1 - n], ups[n])
                south = jnp.where(bottom, downs[1 - n], downs[n])
                m = here[n]
                across = (north + south) + (behind[n] + ahead[n]) - 4.0 * m
                aux = grid[r, now, 1, slot]
                vertical = down(aux)
                extra = source[r, pl.ds(w * ROWS, ROWS), :]
                hor, cpl, ver = (coefs[k, slot] for k in range(3))
                grid[r, then, 0, slot] = 2.0 * m - grid[r, then, 0, slot] + hor * across + cpl * vertical + extra
                grid[r, then, 1, slot] = 2.0 * aux - grid[r, then, 1, slot] + cpl * across + ver * vertical + extra

    def first_merge():
        for s in range(shots):
            for side in range(2):
                @pl.when(yside[side])
                def _(side=side, s=s):
                    first_y(s, side, True).wait_recv()
                    first_y(s, side).wait_send()
            for c in corners:
                @pl.when(cthere[c])
                def _(c=c, s=s):
                    first_d(s, c, True).wait_recv()
                    first_d(s, c).wait_send()
        for side in range(2):
            @pl.when(xside[side])
            def _(side=side):
                for s, n in firsts:
                    first_x(side, s, n, True).wait_recv()
                    first_x(side, s, n).wait_send()

        for s in range(shots):
            for x in range(tx):
                below, above = iy[s, 0, x], iy[s, 1, x]

                def field(n, below=below, above=above):
                    if n == 0:
                        return jnp.where(upper, above, below)
                    return jnp.where(upper, turn(above, -n - 1), turn(below, n + 1))

                for n in range(4):
                    sh[2 * s, n // 2, n % 2, PAIR + x] = field(n)
                if s == 0:
                    parts = mix(*(jnp.where(top | bottom, field(4 + n), 0.0) for n in range(3)))
                    for n in range(3):
                        ch[n, PAIR + x] = parts[n]
        for side in range(2):
            @pl.when(xside[side])
            def _(side=side):
                near, low = (right, right) if side else (1, 0)
                for s in range(shots):
                    for n in range(PAIR):
                        sg[2 * s, 0, 0, low + n] = ix[side, s, n]
                    for n in range(1, 4):
                        sg[2 * s, n // 2, n % 2, near] = ix[side, s, n + 1]
                    sh[2 * s, 0, 0, near] = jnp.where(upper, idg[s, side, 1], idg[s, side, 0])
                parts = mix(ixc[side, 0], ixc[side, 1], ixc[side, 2])
                for n in range(3):
                    cg[n, near] = parts[n]

    def halo_x(slot, r, side, n, arrival=False):
        if n == 0:
            rows, target = pl.ds(right - PAIR if side else PAIR, PAIR), pl.ds(0, PAIR)
        else:
            rows, target = pl.ds(right - 1 if side else PAIR, 1), pl.ds(PAIR, 1)
        into = side if arrival else 1 - side
        target = rx.at[slot, r, into, target]
        return pltpu.make_async_remote_copy(
            src_ref=target if arrival else sg.at[r, 0, n, rows], dst_ref=target, send_sem=hsx.at[slot, r, side, n],
            recv_sem=hrx.at[slot, r, into, n], device_id=xdev[side], device_id_type=MESH,
        )

    def halo_y(slot, r, side, arrival=False):
        into = side if arrival else 1 - side
        target = ry.at[slot, r, into]
        return pltpu.make_async_remote_copy(
            src_ref=target if arrival else py.at[r, side], dst_ref=target, send_sem=hsy.at[slot, r, side],
            recv_sem=hry.at[slot, r, into], device_id=ydev[side], device_id_type=MESH,
        )

    def halo_d(slot, r, corner, arrival=False):
        i, j = corner
        u, v = corner if arrival else (1 - i, 1 - j)
        target = rd.at[slot, r, u, v]
        return pltpu.make_async_remote_copy(
            src_ref=target if arrival else pc.at[r, i, j], dst_ref=target,
            send_sem=hsd.at[slot, r, i, j], recv_sem=hrd.at[slot, r, u, v], device_id=cdev[corner],
            device_id_type=MESH,
        )

    def corner(slot, r, side):
        above, below = (jnp.broadcast_to(rd[slot, r, side, n], (ROWS, nz)) for n in (1, 0))
        return jnp.where(upper, above, below)

    def merge(slot, r):
        for side in range(2):
            @pl.when(yside[side])
            def _(side=side):
                halo_y(slot, r, side, True).wait_recv()
                halo_y(slot, r, side).wait_send()
        for x in range(tx):
            n, k = x // quad, x % quad
            sh[r, 0, 0, PAIR + x] = jnp.where(
                upper, turn(ry[slot, r, 1, n], -PAIR * k), turn(ry[slot, r, 0, n], -PAIR * (k + 1))
            )
            n, k = mains + x // ROWS, x % ROWS
            sh[r, 0, 1, PAIR + x] = jnp.where(upper, turn(ry[slot, r, 1, n], -k), turn(ry[slot, r, 0, n], -k - 1))
        for c in corners:
            @pl.when(cthere[c])
            def _(c=c):
                halo_d(slot, r, c, True).wait_recv()
                halo_d(slot, r, c).wait_send()
        for side in range(2):
            @pl.when(xside[side])
            def _(side=side):
                for n in range(2):
                    halo_x(slot, r, side, n, True).wait_recv()
                    halo_x(slot, r, side, n).wait_send()
                near, low = (right, right) if side else (1, 0)
                for n in range(PAIR):
                    sg[r, 0, 0, low + n] = rx[slot, r, side, n]
                sg[r, 0, 1, near] = rx[slot, r, side, PAIR]
                sh[r, 0, 0, near] = corner(slot, r, side)

    def send_x(slot, r):
        for i, j in corners:
            v = sg[r, 0, 0, right - 1 if i else PAIR]
            pc[r, i, j] = v[ROWS - 1:] if j else v[:1]
        for c in corners:
            @pl.when(cthere[c])
            def _(c=c):
                halo_d(slot, r, c).start()
        for side in range(2):
            @pl.when(xside[side])
            def _(side=side):
                for n in range(2):
                    halo_x(slot, r, side, n).start()

    def send_y(slot, r):
        for n in range(packs):
            field, size, first = (0, PAIR, n * quad) if n < mains else (1, 1, (n - mains) * ROWS)
            lower = higher = None
            for k in range(ROWS // size):
                v = sg[r, 0, field, PAIR + first + k]
                one, two = turn(v, size * k), turn(v, size * (k + 1))
                lower = one if k == 0 else jnp.where(row < size * k, lower, one)
                higher = two if k == 0 else jnp.where(row < size * k, higher, two)
            py[r, 0, n] = lower
            py[r, 1, n] = higher
        for side in range(2):
            @pl.when(yside[side])
            def _(side=side):
                halo_y(slot, r, side).start()

    def fringe_copy(j, s, side, arrival=False):
        into = side if arrival else 1 - side
        both = pl.ds(2 * s, 2)
        target = fringe.at[j, into, both]
        return pltpu.make_async_remote_copy(
            src_ref=target if arrival else snaps.at[j, both, pl.ds(tx, HMAX) if side else pl.ds(HMAX, HMAX)],
            dst_ref=target, send_sem=xs.at[j, s, side], recv_sem=xr.at[j, s, into], device_id=xdev[side],
            device_id_type=MESH,
        )

    def send_fringe(j, s):
        for side in range(2):
            @pl.when(xside[side])
            def _(side=side):
                fringe_copy(j, s, side).start()

    def merge_fringe(j, carry):
        for s in range(shots):
            for side in range(2):
                @pl.when(xside[side])
                def _(side=side, s=s):
                    fringe_copy(j, s, side, True).wait_recv()
                    fringe_copy(j, s, side).wait_send()
                    for r in range(2 * s, 2 * s + 2):
                        for x in range(HMAX):
                            snaps[j, r, side * (HMAX + tx) + x] = fringe[j, side, r, x]
        return carry

    brink = list(range(PAIR)) + list(range(tx - PAIR, tx))
    rest = list(range(PAIR, tx - PAIR))

    def cycle(e, carry):
        for r in range(waves):
            inject(e, r)

        @pl.when(e == 0)
        def _():
            first_merge()

        for r in range(waves):
            @pl.when(e > 0)
            def _(r=r):
                merge(e % 2, r)

            advance(r, 0, start, range(width), True, injg, injh)
            advance(r, 1, PAIR, brink, False, injb, None)

            @pl.when(e < turns - 1)
            def _(r=r):
                send_x((e + 1) % 2, r)

            advance(r, 1, PAIR, rest, False, injb, None)

            @pl.when(e < turns - 1)
            def _(r=r):
                send_y((e + 1) % 2, r)

        @pl.when(e % per == per - 1)
        def _():
            j = e // per
            for r in range(waves):
                for x in range(tx):
                    snaps[j, r, HMAX + x] = sg[r, 0, 0, PAIR + x]
            send_fringe(j, 0)

        @pl.when(e == turns - 1)
        def _():
            for s in range(1, shots):
                send_fringe(blocks - 1, s)

        @pl.when((e % per == 0) & (e > 0))
        def _():
            for s in range(1, shots):
                send_fringe(e // per - 1, s)

        return carry

    lax.fori_loop(0, turns, cycle, 0)

    def swap_copy(n, rows, part):
        return pltpu.make_async_remote_copy(
            src_ref=outgoing.at[n, rows], dst_ref=out.at[n, rows, mine, :], send_sem=gs.at[part, n],
            recv_sem=gr.at[part, n], device_id=partner, device_id_type=MESH,
        )

    def product(shift, x):
        sums = None
        for j in range(blocks):
            for s in range(shots):
                term = snaps[j, 2 * s, HMAX - shift + x] * snaps[j, 2 * s + 1, HMAX + shift + x]
                sums = term if sums is None else sums + term
        return sums

    mid = tx // 2
    spans = [pl.ds(a * mid, mid), pl.ds((1 - a) * mid, mid)] if nx == 2 else [pl.ds(0, mid), pl.ds(mid, mid)]
    for part, rows in enumerate(spans):
        if part == (1 if nx == 2 else 0):
            lax.fori_loop(0, blocks, merge_fringe, 0)

        def theirs(n, carry, part=part, rows=rows):
            shift = offsets[pair * own + (1 - half) * own + n]
            for x in range(mid):
                outgoing[n, rows.start + x] = product(shift, rows.start + x)
            swap_copy(n, rows, part).start()
            return carry

        lax.fori_loop(0, own, theirs, 0)

    def ours(n, carry):
        shift = offsets[pair * own + half * own + n]
        for x in range(tx):
            out[n, x, mine, :] = product(shift, x)
        return carry

    lax.fori_loop(0, own, ours, 0)
    for part, rows in enumerate(spans):
        def done(n, carry, part=part, rows=rows):
            swap_copy(n, rows, part).wait_recv()
            swap_copy(n, rows, part).wait_send()
            return carry

        lax.fori_loop(0, own, done, 0)


def shards(sizes, checkpoint, courant, epsilon, delta, positions, amplitudes, offsets):
    ng, nx, ny = sizes
    shots = checkpoint.shape[0]
    waves = 2 * shots
    tx, ty, nz = courant.shape
    nrec = positions.shape[2]
    steps = amplitudes.shape[1]
    blocks = steps // SNAP
    nh = offsets.shape[0]
    own = nh // ng
    assert ng % 2 == 0 and ty == 2 * ROWS and tx == 2 * HMAX and nz % LANES == 0 and nh % ng == 0 and nx > 1
    assert shots <= 2 and steps % SNAP == 0
    width = tx + (1 if nx == 2 else 2)
    wide = (width + 1) // 2 * 2 * ROWS
    slots = tx + 2 * PAIR
    packs = tx * PAIR // ROWS + tx // ROWS
    f32, bf16 = jnp.float32, jnp.bfloat16
    dma = pltpu.SemaphoreType.DMA
    vmem = pl.BlockSpec(memory_space=pltpu.VMEM)
    anywhere = pl.BlockSpec(memory_space=pl.ANY)

    def held(*shape, dtype=f32):
        return pltpu.VMEM(shape, dtype)

    return pl.pallas_call(
        functools.partial(kernel, sizes),
        out_shape=jax.ShapeDtypeStruct((own, tx, ty, nz), f32),
        in_specs=[anywhere] * 4 + [vmem] * 2 + [pl.BlockSpec(memory_space=pltpu.SMEM)],
        out_specs=vmem,
        scratch_shapes=[
            held(waves, 2, 2, slots, ROWS, nz),
            held(waves, 2, 2, slots, ROWS, nz),
            held(3, tx, ROWS, nz),
            held(3, slots, ROWS, nz),
            held(3, slots, ROWS, nz),
            held(waves, wide, nrec, dtype=bf16),
            held(waves, wide, nrec, dtype=bf16),
            held(waves, tx * ROWS, nrec, dtype=bf16),
            held(waves, 2 * nrec, nz, dtype=bf16),
            held(waves, wide, nz),
            held(waves, wide, nz),
            held(waves, tx * ROWS, nz),
            held(2, shots, PAIR + 3, ROWS, nz),
            held(2, 3, ROWS, nz),
            held(shots, 2, tx, ROWS, nz),
            held(shots, 2, 2, ROWS, nz),
            held(shots, 2, tx, ROWS, nz),
            held(waves, 2, packs, ROWS, nz),
            held(waves, 2, 2, 1, nz),
            held(2, waves, 2, PAIR + 1, ROWS, nz),
            held(2, waves, 2, packs, ROWS, nz),
            held(2, waves, 2, 2, 1, nz),
            held(blocks, waves, tx + 2 * HMAX, ROWS, nz),
            held(blocks, 2, waves, HMAX, ROWS, nz),
            held(own, tx, ROWS, nz),
            dma((3 + 4 * shots,)),
            dma((2, shots + 1, 4)),
            dma((2, shots + 1, 4)),
            dma((shots, 2)),
            dma((shots, 2)),
            dma((shots, 2, 2)),
            dma((shots, 2, 2)),
            dma((2, waves, 2, 2)),
            dma((2, waves, 2, 2)),
            dma((2, waves, 2)),
            dma((2, waves, 2)),
            dma((2, waves, 2, 2)),
            dma((2, waves, 2, 2)),
            dma((blocks, shots, 2)),
            dma((blocks, shots, 2)),
            dma((2, own)),
            dma((2, own)),
        ],
        compiler_params=pltpu.CompilerParams(
            collective_id=0, has_side_effects=True, vmem_limit_bytes=58720256
        ),
    )(courant, epsilon, delta, checkpoint, positions.transpose(1, 0, 2), amplitudes, offsets)


def solution(mesh):
    sizes = tuple(mesh.shape[axis] for axis in ("grp", "gx", "gy"))
    return jax.shard_map(
        functools.partial(shards, sizes),
        mesh=mesh,
        in_specs=(
            P(None, None, None, "gx", "gy", None),
            P("gx", "gy", None),
            P("gx", "gy", None),
            P("gx", "gy", None),
            P(),
            P(),
            P(),
        ),
        out_specs=P("grp", "gx", "gy", None),
        check_vma=False,
    )
```

time: 77.8 us -> 68.9 us (0.89)
  Pallas kernels: 75.3 us -> 66.4 us
    pallas_call x1, Pallas kernels: 75.3 us -> 66.4 us  [shards(): pl.pallas_call(functools.partial(kernel, sizes), out_shape=jax.ShapeDtype...]
where the time goes in v3:
time: 68.9 us; the launch traced here: 68.7 us
  Pallas kernels  66.4 us (96%)
  local copies, waits for them, and re-layouts  2.26 us (3%)
    pallas_call x1, Pallas kernels, shards(): pl.pallas_call(functools.partial(kernel, sizes), out_shape=jax.ShapeDtype...  66.4 us
    unnamed x1, local copies, waits for them, and re-layouts  2.26 us

profile of v3, /device:TPU:0, one launch (start us, length us, event | category | flops | bytes accessed | tf_op | source)
XLA Modules:
  0.0 68.7 jit_solution(13454707297310488268)
XLA Ops:
  0.0 66.4 %shard_map.73 = f32[4,16,16,256]{3,2,1,0:T(8,128)} custom-call(f32[16,16,256]{2,1,0:T(8,128)} %courant.1, f32[16,16,256]{2,1,0:T(8,128)} %epsilon.1, f32[16,16,256]{2,1,0:T(8,128)} %delta.1, f32[2,2,2,16,16,256]{5,4,3,2,1,0:T(8,128)} %checkpoint.1, s32[3,4,512]{2,1,0:T(4,128)} %bitcast.1, f32[4,16,512]{2,1,0:T(8,128)} %amplitudes.1, s32[16]{0:T(128)} %offsets.1), custom_call_target="tpu_custom_call" | custom-call | tf_op jit(solution)/shard_map/pallas_call | solution.py:583
  66.4 2.3 %copy.9 = f32[4,16,16,256]{3,2,1,0:T(8,128)} copy(f32[4,16,16,256]{3,2,1,0:T(8,128)} %shard_map.73) | data formatting | bytes 2097152

commit v4 on v3

--- a/solution.py
+++ b/solution.py
@@ -14,8 +14,8 @@
 MESH = pl.DeviceIdType.MESH
 
 
-def kernel(sizes, courant, epsilon, delta, checkpoint, positions, amplitudes, offsets, out,
-           sg, sh, raw, cg, ch, pickg, pickh, pickb, spot, injg, injh, injb, ix, ixc, iy, idg, pi, py, pc, rx, ry, rd,
+def kernel(sizes, courant, epsilon, delta, checkpoint, places, weights, shifts, out,
+           positions, amplitudes, offsets, sg, sh, raw, cg, ch, pickg, pickh, pickb, spot, injg, injh, injb, ix, ixc, iy, idg, pi, py, pc, rx, ry, rd,
            snaps, fringe, outgoing,
            ls, isx, irx, isy, iry, isd, ird, hsx, hrx, hsy, hry, hsd, hrd, xs, xr, gs, gr):
     ng, nx, ny = sizes
@@ -73,10 +73,16 @@
         )
 
     loads = [(s, moment, field) for s in range(shots) for moment in range(2) for field in range(2)]
+    tables = [
+        pltpu.make_async_copy(source, target, ls.at[3 + 4 * shots + n])
+        for n, (source, target) in enumerate(((places, positions), (weights, amplitudes), (shifts, offsets)))
+    ]
     for n in range(3):
         model_load(n).start()
     for load in loads:
         state_load(*load).start()
+    for table in tables:
+        table.start()
 
     zero = jnp.zeros((ROWS, nz), f32)
     row = lax.broadcasted_iota(jnp.int32, (ROWS, nz), 0)
@@ -201,6 +207,8 @@
         for n in range(3):
             cg[n, PAIR + x] = parts[n]
 
+    for table in tables:
+        table.wait()
     tile = 2 * ROWS
     wide = (width * ROWS + tile - 1) // tile
     count = lax.broadcasted_iota(jnp.int32, (tile, nrec), 0)
@@ -290,53 +298,49 @@
                 grid[r, then, 0, slot] = 2.0 * m - grid[r, then, 0, slot] + hor * across + cpl * vertical + extra
                 grid[r, then, 1, slot] = 2.0 * aux - grid[r, then, 1, slot] + cpl * across + ver * vertical + extra
 
-    def first_merge():
-        for s in range(shots):
-            for side in range(2):
-                @pl.when(yside[side])
-                def _(side=side, s=s):
-                    first_y(s, side, True).wait_recv()
-                    first_y(s, side).wait_send()
-            for c in corners:
-                @pl.when(cthere[c])
-                def _(c=c, s=s):
-                    first_d(s, c, True).wait_recv()
-                    first_d(s, c).wait_send()
+    def first_merge(s):
+        for side in range(2):
+            @pl.when(yside[side])
+            def _(side=side):
+                first_y(s, side, True).wait_recv()
+                first_y(s, side).wait_send()
+        for c in corners:
+            @pl.when(cthere[c])
+            def _(c=c):
+                first_d(s, c, True).wait_recv()
+                first_d(s, c).wait_send()
+
+        for x in range(tx):
+            below, above = iy[s, 0, x], iy[s, 1, x]
+
+            def field(n, below=below, above=above):
+                if n == 0:
+                    return jnp.where(upper, above, below)
+                return jnp.where(upper, turn(above, -n - 1), turn(below, n + 1))
+
+            for n in range(4):
+                sh[2 * s, n // 2, n % 2, PAIR + x] = field(n)
+            if s == 0:
+                parts = mix(*(jnp.where(top | bottom, field(4 + n), 0.0) for n in range(3)))
+                for n in range(3):
+                    ch[n, PAIR + x] = parts[n]
         for side in range(2):
             @pl.when(xside[side])
             def _(side=side):
-                for s, n in firsts:
-                    first_x(side, s, n, True).wait_recv()
-                    first_x(side, s, n).wait_send()
-
-        for s in range(shots):
-            for x in range(tx):
-                below, above = iy[s, 0, x], iy[s, 1, x]
-
-                def field(n, below=below, above=above):
-                    if n == 0:
-                        return jnp.where(upper, above, below)
-                    return jnp.where(upper, turn(above, -n - 1), turn(below, n + 1))
-
-                for n in range(4):
-                    sh[2 * s, n // 2, n % 2, PAIR + x] = field(n)
+                for group, n in firsts:
+                    if group == s or (s == 0 and group == shots):
+                        first_x(side, group, n, True).wait_recv()
+                        first_x(side, group, n).wait_send()
+                near, low = (right, right) if side else (1, 0)
+                for n in range(PAIR):
+                    sg[2 * s, 0, 0, low + n] = ix[side, s, n]
+                for n in range(1, 4):
+                    sg[2 * s, n // 2, n % 2, near] = ix[side, s, n + 1]
+                sh[2 * s, 0, 0, near] = jnp.where(upper, idg[s, side, 1], idg[s, side, 0])
                 if s == 0:
-                    parts = mix(*(jnp.where(top | bottom, field(4 + n), 0.0) for n in range(3)))
+                    parts = mix(ixc[side, 0], ixc[side, 1], ixc[side, 2])
                     for n in range(3):
-                        ch[n, PAIR + x] = parts[n]
-        for side in range(2):
-            @pl.when(xside[side])
-            def _(side=side):
-                near, low = (right, right) if side else (1, 0)
-                for s in range(shots):
-                    for n in range(PAIR):
-                        sg[2 * s, 0, 0, low + n] = ix[side, s, n]
-                    for n in range(1, 4):
-                        sg[2 * s, n // 2, n % 2, near] = ix[side, s, n + 1]
-                    sh[2 * s, 0, 0, near] = jnp.where(upper, idg[s, side, 1], idg[s, side, 0])
-                parts = mix(ixc[side, 0], ixc[side, 1], ixc[side, 2])
-                for n in range(3):
-                    cg[n, near] = parts[n]
+                        cg[n, near] = parts[n]
 
     def halo_x(slot, r, side, n, arrival=False):
         if n == 0:
@@ -467,11 +471,12 @@
         for r in range(waves):
             inject(e, r)
 
-        @pl.when(e == 0)
-        def _():
-            first_merge()
-
         for r in range(waves):
+            if r % 2 == 0:
+                @pl.when(e == 0)
+                def _(r=r):
+                    first_merge(r // 2)
+
             @pl.when(e > 0)
             def _(r=r):
                 merge(e % 2, r)
@@ -489,18 +494,20 @@
             def _(r=r):
                 send_y((e + 1) % 2, r)
 
-        @pl.when(e % per == per - 1)
+            if r % 2 == 1:
+                @pl.when(e % per == per - 1)
+                def _(r=r):
+                    for n in (r - 1, r):
+                        for x in range(tx):
+                            snaps[e // per, n, HMAX + x] = sg[n, 0, 0, PAIR + x]
+
+                @pl.when(e == turns - 1)
+                def _(r=r):
+                    send_fringe(blocks - 1, r // 2)
+
+        @pl.when((e % per == per - 1) & (e < turns - 1))
         def _():
-            j = e // per
-            for r in range(waves):
-                for x in range(tx):
-                    snaps[j, r, HMAX + x] = sg[r, 0, 0, PAIR + x]
-            send_fringe(j, 0)
-
-        @pl.when(e == turns - 1)
-        def _():
-            for s in range(1, shots):
-                send_fringe(blocks - 1, s)
+            send_fringe(e // per, 0)
 
         @pl.when((e % per == 0) & (e > 0))
         def _():
@@ -575,7 +582,9 @@
     f32, bf16 = jnp.float32, jnp.bfloat16
     dma = pltpu.SemaphoreType.DMA
     vmem = pl.BlockSpec(memory_space=pltpu.VMEM)
-    anywhere = pl.BlockSpec(memory_space=pl.ANY)
+
+    places = positions.transpose(1, 0, 2)
+    arguments = (courant, epsilon, delta, checkpoint, places, amplitudes, offsets)
 
     def held(*shape, dtype=f32):
         return pltpu.VMEM(shape, dtype)
@@ -583,9 +592,12 @@
     return pl.pallas_call(
         functools.partial(kernel, sizes),
         out_shape=jax.ShapeDtypeStruct((own, tx, ty, nz), f32),
-        in_specs=[anywhere] * 4 + [vmem] * 2 + [pl.BlockSpec(memory_space=pltpu.SMEM)],
+        in_specs=[pl.BlockSpec(memory_space=pltpu.HBM)] * 7,
         out_specs=vmem,
         scratch_shapes=[
+            held(*places.shape, dtype=places.dtype),
+            held(*amplitudes.shape),
+            pltpu.SMEM(offsets.shape, offsets.dtype),
             held(waves, 2, 2, slots, ROWS, nz),
             held(waves, 2, 2, slots, ROWS, nz),
             held(3, tx, ROWS, nz),
@@ -611,7 +623,7 @@
             held(blocks, waves, tx + 2 * HMAX, ROWS, nz),
             held(blocks, 2, waves, HMAX, ROWS, nz),
             held(own, tx, ROWS, nz),
-            dma((3 + 4 * shots,)),
+            dma((6 + 4 * shots,)),
             dma((2, shots + 1, 4)),
             dma((2, shots + 1, 4)),
             dma((shots, 2)),
@@ -630,9 +642,9 @@
             dma((2, own)),
         ],
         compiler_params=pltpu.CompilerParams(
-            collective_id=0, has_side_effects=True, vmem_limit_bytes=58720256
+            collective_id=0, has_side_effects=True, vmem_limit_bytes=44 * 1024 * 1024
         ),
-    )(courant, epsilon, delta, checkpoint, positions.transpose(1, 0, 2), amplitudes, offsets)
+    )(*(pltpu.with_memory_space_constraint(v, pltpu.HBM) for v in arguments))
 
 
 def solution(mesh):

time: 68.9 us -> 64.2 us (0.932)
  Pallas kernels: 66.4 us -> 63.1 us
  local copies, waits for them, and re-layouts: 2.26 us -> 0.97 us
    pallas_call x1, Pallas kernels: 66.4 us -> 63.1 us  [shards(): pl.pallas_call(functools.partial(kernel, sizes), out_shape=jax.ShapeDtype...]
    unnamed x1, local copies, waits for them, and re-layouts: 2.26 us -> 0.97 us
where the time goes in v4:
time: 64.2 us; the launch traced here: 64.1 us
  Pallas kernels  63.1 us (98%)
  local copies, waits for them, and re-layouts  0.97 us (2%)
    pallas_call x1, Pallas kernels, shards(): pl.pallas_call(functools.partial(kernel, sizes), out_shape=jax.ShapeDtype...  63.1 us

profile of v4, /device:TPU:0, one launch (start us, length us, event | category | flops | bytes accessed | tf_op | source)
XLA Modules:
  0.0 64.1 jit_solution(13531740846526877027)
XLA Ops:
  0.0 63.1 %shard_map.73 = f32[4,16,16,256]{3,2,1,0:T(8,128)S(1)} custom-call(f32[16,16,256]{2,1,0:T(8,128)} %courant.1, f32[16,16,256]{2,1,0:T(8,128)} %epsilon.1, f32[16,16,256]{2,1,0:T(8,128)} %delta.1, f32[2,2,2,16,16,256]{5,4,3,2,1,0:T(8,128)} %checkpoint.1, s32[3,4,512]{2,1,0:T(4,128)} %bitcast.1, f32[4,16,512]{2,1,0:T(8,128)} %weights.1, s32[16]{0:T(128)} %shifts.1), custom_call_target="tpu_custom_call" | custom-call | tf_op jit(solution)/shard_map/pallas_call | solution.py:592
  63.1 1.0 %copy.9 = f32[4,16,16,256]{3,2,1,0:T(8,128)} copy(f32[4,16,16,256]{3,2,1,0:T(8,128)S(1)} %shard_map.73) | data formatting | bytes 2097152

commit v5 on v4

--- a/solution.py
+++ b/solution.py
@@ -94,8 +94,7 @@
         return v if shift == 0 else pltpu.roll(v, shift, axis)
 
     outer = (0, 1, right, right + 1)
-    quad, mains = ROWS // PAIR, tx * PAIR // ROWS
-    packs = mains + tx // ROWS
+    quad, packs, strips = ROWS // PAIR, PAIR + 1, tx // ROWS
 
     def wipe(x, carry):
         for r in range(waves):
@@ -121,10 +120,11 @@
             for x in range(tx):
                 for s in range(shots):
                     iy[s, side, x] = zero
-            for n in range(packs):
-                for slot in range(2):
-                    for r in range(waves):
-                        ry[slot, r, side, n] = zero
+            for slot in range(2):
+                for r in range(waves):
+                    for strip in range(strips):
+                        for n in range(packs):
+                            ry[slot, r, side, strip, n] = zero
     for i, j in corners:
         @pl.when(jnp.logical_not(cthere[i, j]))
         def _(i=i, j=j):
@@ -354,12 +354,12 @@
             recv_sem=hrx.at[slot, r, into, n], device_id=xdev[side], device_id_type=MESH,
         )
 
-    def halo_y(slot, r, side, arrival=False):
+    def halo_y(slot, r, side, strip, arrival=False):
         into = side if arrival else 1 - side
-        target = ry.at[slot, r, into]
-        return pltpu.make_async_remote_copy(
-            src_ref=target if arrival else py.at[r, side], dst_ref=target, send_sem=hsy.at[slot, r, side],
-            recv_sem=hry.at[slot, r, into], device_id=ydev[side], device_id_type=MESH,
+        target = ry.at[slot, r, into, strip]
+        return pltpu.make_async_remote_copy(
+            src_ref=target if arrival else py.at[r, side, strip], dst_ref=target, send_sem=hsy.at[slot, r, side, strip],
+            recv_sem=hry.at[slot, r, into, strip], device_id=ydev[side], device_id_type=MESH,
         )
 
     def halo_d(slot, r, corner, arrival=False):
@@ -380,15 +380,16 @@
         for side in range(2):
             @pl.when(yside[side])
             def _(side=side):
-                halo_y(slot, r, side, True).wait_recv()
-                halo_y(slot, r, side).wait_send()
+                for strip in range(strips):
+                    halo_y(slot, r, side, strip, True).wait_recv()
+                    halo_y(slot, r, side, strip).wait_send()
         for x in range(tx):
-            n, k = x // quad, x % quad
-            sh[r, 0, 0, PAIR + x] = jnp.where(
-                upper, turn(ry[slot, r, 1, n], -PAIR * k), turn(ry[slot, r, 0, n], -PAIR * (k + 1))
-            )
-            n, k = mains + x // ROWS, x % ROWS
-            sh[r, 0, 1, PAIR + x] = jnp.where(upper, turn(ry[slot, r, 1, n], -k), turn(ry[slot, r, 0, n], -k - 1))
+            strip, w = x // ROWS, x % ROWS
+            n, k = w // quad, w % quad
+            below, above = ry[slot, r, 0, strip, n], ry[slot, r, 1, strip, n]
+            sh[r, 0, 0, PAIR + x] = jnp.where(upper, turn(above, -PAIR * k), turn(below, -PAIR * (k + 1)))
+            below, above = ry[slot, r, 0, strip, PAIR], ry[slot, r, 1, strip, PAIR]
+            sh[r, 0, 1, PAIR + x] = jnp.where(upper, turn(above, -w), turn(below, -w - 1))
         for c in corners:
             @pl.when(cthere[c])
             def _(c=c):
@@ -420,52 +421,58 @@
                 for n in range(2):
                     halo_x(slot, r, side, n).start()
 
-    def send_y(slot, r):
+    def send_y(slot, r, strip):
         for n in range(packs):
-            field, size, first = (0, PAIR, n * quad) if n < mains else (1, 1, (n - mains) * ROWS)
+            field, size, first = (0, PAIR, n * quad) if n < PAIR else (1, 1, 0)
             lower = higher = None
             for k in range(ROWS // size):
-                v = sg[r, 0, field, PAIR + first + k]
+                v = sg[r, 0, field, PAIR + strip * ROWS + first + k]
                 one, two = turn(v, size * k), turn(v, size * (k + 1))
                 lower = one if k == 0 else jnp.where(row < size * k, lower, one)
                 higher = two if k == 0 else jnp.where(row < size * k, higher, two)
-            py[r, 0, n] = lower
-            py[r, 1, n] = higher
+            py[r, 0, strip, n] = lower
+            py[r, 1, strip, n] = higher
         for side in range(2):
             @pl.when(yside[side])
             def _(side=side):
-                halo_y(slot, r, side).start()
-
-    def fringe_copy(j, s, side, arrival=False):
+                halo_y(slot, r, side, strip).start()
+
+    def fringe_copy(j, s, side, skip, arrival=False):
         into = side if arrival else 1 - side
         both = pl.ds(2 * s, 2)
-        target = fringe.at[j, into, both]
-        return pltpu.make_async_remote_copy(
-            src_ref=target if arrival else snaps.at[j, both, pl.ds(tx, HMAX) if side else pl.ds(HMAX, HMAX)],
-            dst_ref=target, send_sem=xs.at[j, s, side], recv_sem=xr.at[j, s, into], device_id=xdev[side],
-            device_id_type=MESH,
-        )
-
-    def send_fringe(j, s):
+        target = fringe.at[j, into, both, pl.ds(0, HMAX - skip)]
+        source = pl.ds(tx if side else HMAX + skip, HMAX - skip)
+        return pltpu.make_async_remote_copy(
+            src_ref=target if arrival else snaps.at[j, both, source], dst_ref=target, send_sem=xs.at[j, s, side],
+            recv_sem=xr.at[j, s, into], device_id=xdev[side], device_id_type=MESH,
+        )
+
+    def send_fringe(j, s, skip):
         for side in range(2):
             @pl.when(xside[side])
             def _(side=side):
-                fringe_copy(j, s, side).start()
-
-    def merge_fringe(j, carry):
+                fringe_copy(j, s, side, skip).start()
+
+    def merge_fringe(j, skip):
         for s in range(shots):
             for side in range(2):
                 @pl.when(xside[side])
                 def _(side=side, s=s):
-                    fringe_copy(j, s, side, True).wait_recv()
-                    fringe_copy(j, s, side).wait_send()
+                    fringe_copy(j, s, side, skip, True).wait_recv()
+                    fringe_copy(j, s, side, skip).wait_send()
                     for r in range(2 * s, 2 * s + 2):
-                        for x in range(HMAX):
-                            snaps[j, r, side * (HMAX + tx) + x] = fringe[j, side, r, x]
-        return carry
+                        for x in range(HMAX - skip):
+                            snaps[j, r, side * (HMAX + tx + skip) + x] = fringe[j, side, r, x]
+
+    def keep_halo(e, r):
+        for side in range(2):
+            @pl.when(xside[side])
+            def _(side=side):
+                for n in range(PAIR):
+                    snaps[e // per - 1, r, (HMAX + tx if side else HMAX - PAIR) + n] = rx[e % 2, r, side, n]
 
     brink = list(range(PAIR)) + list(range(tx - PAIR, tx))
-    rest = list(range(PAIR, tx - PAIR))
+    rest = [[x for x in range(n * ROWS, (n + 1) * ROWS) if x not in brink] for n in range(strips)]
 
     def cycle(e, carry):
         for r in range(waves):
@@ -481,6 +488,10 @@
             def _(r=r):
                 merge(e % 2, r)
 
+            @pl.when((e % per == 0) & (e > 0))
+            def _(r=r):
+                keep_halo(e, r)
+
             advance(r, 0, start, range(width), True, injg, injh)
             advance(r, 1, PAIR, brink, False, injb, None)
 
@@ -488,11 +499,12 @@
             def _(r=r):
                 send_x((e + 1) % 2, r)
 
-            advance(r, 1, PAIR, rest, False, injb, None)
-
-            @pl.when(e < turns - 1)
-            def _(r=r):
-                send_y((e + 1) % 2, r)
+            for strip in range(strips):
+                advance(r, 1, PAIR, rest[strip], False, injb, None)
+
+                @pl.when(e < turns - 1)
+                def _(r=r, strip=strip):
+                    send_y((e + 1) % 2, r, strip)
 
             if r % 2 == 1:
                 @pl.when(e % per == per - 1)
@@ -503,16 +515,16 @@
 
                 @pl.when(e == turns - 1)
                 def _(r=r):
-                    send_fringe(blocks - 1, r // 2)
+                    send_fringe(blocks - 1, r // 2, 0)
 
         @pl.when((e % per == per - 1) & (e < turns - 1))
         def _():
-            send_fringe(e // per, 0)
+            send_fringe(e // per, 0, PAIR)
 
         @pl.when((e % per == 0) & (e > 0))
         def _():
             for s in range(1, shots):
-                send_fringe(e // per - 1, s)
+                send_fringe(e // per - 1, s, PAIR)
 
         return carry
 
@@ -536,7 +548,12 @@
     spans = [pl.ds(a * mid, mid), pl.ds((1 - a) * mid, mid)] if nx == 2 else [pl.ds(0, mid), pl.ds(mid, mid)]
     for part, rows in enumerate(spans):
         if part == (1 if nx == 2 else 0):
-            lax.fori_loop(0, blocks, merge_fringe, 0)
+            def earlier(j, carry):
+                merge_fringe(j, PAIR)
+                return carry
+
+            lax.fori_loop(0, blocks - 1, earlier, 0)
+            merge_fringe(blocks - 1, 0)
 
         def theirs(n, carry, part=part, rows=rows):
             shift = offsets[pair * own + (1 - half) * own + n]
@@ -578,7 +595,7 @@
     width = tx + (1 if nx == 2 else 2)
     wide = (width + 1) // 2 * 2 * ROWS
     slots = tx + 2 * PAIR
-    packs = tx * PAIR // ROWS + tx // ROWS
+    packs, strips = PAIR + 1, tx // ROWS
     f32, bf16 = jnp.float32, jnp.bfloat16
     dma = pltpu.SemaphoreType.DMA
     vmem = pl.BlockSpec(memory_space=pltpu.VMEM)
@@ -615,10 +632,10 @@
             held(shots, 2, tx, ROWS, nz),
             held(shots, 2, 2, ROWS, nz),
             held(shots, 2, tx, ROWS, nz),
-            held(waves, 2, packs, ROWS, nz),
+            held(waves, 2, strips, packs, ROWS, nz),
             held(waves, 2, 2, 1, nz),
             held(2, waves, 2, PAIR + 1, ROWS, nz),
-            held(2, waves, 2, packs, ROWS, nz),
+            held(2, waves, 2, strips, packs, ROWS, nz),
             held(2, waves, 2, 2, 1, nz),
             held(blocks, waves, tx + 2 * HMAX, ROWS, nz),
             held(blocks, 2, waves, HMAX, ROWS, nz),
@@ -632,8 +649,8 @@
             dma((shots, 2, 2)),
             dma((2, waves, 2, 2)),
             dma((2, waves, 2, 2)),
-            dma((2, waves, 2)),
-            dma((2, waves, 2)),
+            dma((2, waves, 2, strips)),
+            dma((2, waves, 2, strips)),
             dma((2, waves, 2, 2)),
             dma((2, waves, 2, 2)),
             dma((blocks, shots, 2)),

time: 64.2 us -> 60.9 us (0.949)
  Pallas kernels: 63.1 us -> 59.8 us
    pallas_call x1, Pallas kernels: 63.1 us -> 59.8 us  [shards(): pl.pallas_call(functools.partial(kernel, sizes), out_shape=jax.ShapeDtype...]
where the time goes in v5:
time: 60.9 us; the launch traced here: 60.8 us
  Pallas kernels  59.8 us (98%)
  local copies, waits for them, and re-layouts  0.97 us (2%)
    pallas_call x1, Pallas kernels, shards(): pl.pallas_call(functools.partial(kernel, sizes), out_shape=jax.ShapeDtype...  59.8 us

profile of v5, /device:TPU:0, one launch (start us, length us, event | category | flops | bytes accessed | tf_op | source)
XLA Modules:
  0.0 60.8 jit_solution(6890641350383463698)
XLA Ops:
  0.0 59.8 %shard_map.73 = f32[4,16,16,256]{3,2,1,0:T(8,128)S(1)} custom-call(f32[16,16,256]{2,1,0:T(8,128)} %courant.1, f32[16,16,256]{2,1,0:T(8,128)} %epsilon.1, f32[16,16,256]{2,1,0:T(8,128)} %delta.1, f32[2,2,2,16,16,256]{5,4,3,2,1,0:T(8,128)} %checkpoint.1, s32[3,4,512]{2,1,0:T(4,128)} %bitcast.1, f32[4,16,512]{2,1,0:T(8,128)} %weights.1, s32[16]{0:T(128)} %shifts.1), custom_call_target="tpu_custom_call" | custom-call | tf_op jit(solution)/shard_map/pallas_call | solution.py:609
  59.8 1.0 %copy.9 = f32[4,16,16,256]{3,2,1,0:T(8,128)} copy(f32[4,16,16,256]{3,2,1,0:T(8,128)S(1)} %shard_map.73) | data formatting | bytes 2097152

commit v6 on v5

--- a/solution.py
+++ b/solution.py
@@ -471,6 +471,7 @@
                 for n in range(PAIR):
                     snaps[e // per - 1, r, (HMAX + tx if side else HMAX - PAIR) + n] = rx[e % 2, r, side, n]
 
+    queue = [0, 1] + [r for s in range(1, shots) for r in (2 * s + 1, 2 * s)]
     brink = list(range(PAIR)) + list(range(tx - PAIR, tx))
     rest = [[x for x in range(n * ROWS, (n + 1) * ROWS) if x not in brink] for n in range(strips)]
 
@@ -478,7 +479,7 @@
         for r in range(waves):
             inject(e, r)
 
-        for r in range(waves):
+        for place, r in enumerate(queue):
             if r % 2 == 0:
                 @pl.when(e == 0)
                 def _(r=r):
@@ -506,10 +507,10 @@
                 def _(r=r, strip=strip):
                     send_y((e + 1) % 2, r, strip)
 
-            if r % 2 == 1:
+            if place % 2 == 1:
                 @pl.when(e % per == per - 1)
                 def _(r=r):
-                    for n in (r - 1, r):
+                    for n in (r - r % 2, r - r % 2 + 1):
                         for x in range(tx):
                             snaps[e // per, n, HMAX + x] = sg[n, 0, 0, PAIR + x]
 

time: 60.9 us -> 60.4 us (level)
  no operation moved by 1% of the time
where the time goes in v6:
time: 60.4 us; the launch traced here: 60.3 us
  Pallas kernels  59.3 us (98%)
  local copies, waits for them, and re-layouts  0.97 us (2%)
    pallas_call x1, Pallas kernels, shards(): pl.pallas_call(functools.partial(kernel, sizes), out_shape=jax.ShapeDtype...  59.3 us

profile of v6, /device:TPU:0, one launch (start us, length us, event | category | flops | bytes accessed | tf_op | source)
XLA Modules:
  0.0 60.3 jit_solution(13795045845503078396)
XLA Ops:
  0.0 59.3 %shard_map.73 = f32[4,16,16,256]{3,2,1,0:T(8,128)S(1)} custom-call(f32[16,16,256]{2,1,0:T(8,128)} %courant.1, f32[16,16,256]{2,1,0:T(8,128)} %epsilon.1, f32[16,16,256]{2,1,0:T(8,128)} %delta.1, f32[2,2,2,16,16,256]{5,4,3,2,1,0:T(8,128)} %checkpoint.1, s32[3,4,512]{2,1,0:T(4,128)} %bitcast.1, f32[4,16,512]{2,1,0:T(8,128)} %weights.1, s32[16]{0:T(128)} %shifts.1), custom_call_target="tpu_custom_call" | custom-call | tf_op jit(solution)/shard_map/pallas_call | solution.py:610
  59.3 1.0 %copy.9 = f32[4,16,16,256]{3,2,1,0:T(8,128)} copy(f32[4,16,16,256]{3,2,1,0:T(8,128)S(1)} %shard_map.73) | data formatting | bytes 2097152

commit v7 on v6

--- a/solution.py
+++ b/solution.py
@@ -493,19 +493,26 @@
             def _(r=r):
                 keep_halo(e, r)
 
-            advance(r, 0, start, range(width), True, injg, injh)
-            advance(r, 1, PAIR, brink, False, injb, None)
+            cut = ROWS + 2
+            advance(r, 0, start, range(cut), True, injg, injh)
+            advance(r, 1, PAIR, range(ROWS), False, injb, None)
+
+            @pl.when(e < turns - 1)
+            def _(r=r):
+                send_y((e + 1) % 2, r, 0)
+
+            advance(r, 0, start, range(cut, width), True, injg, injh)
+            advance(r, 1, PAIR, range(tx - PAIR, tx), False, injb, None)
 
             @pl.when(e < turns - 1)
             def _(r=r):
                 send_x((e + 1) % 2, r)
 
-            for strip in range(strips):
-                advance(r, 1, PAIR, rest[strip], False, injb, None)
-
-                @pl.when(e < turns - 1)
-                def _(r=r, strip=strip):
-                    send_y((e + 1) % 2, r, strip)
+            advance(r, 1, PAIR, range(ROWS, tx - PAIR), False, injb, None)
+
+            @pl.when(e < turns - 1)
+            def _(r=r):
+                send_y((e + 1) % 2, r, 1)
 
             if place % 2 == 1:
                 @pl.when(e % per == per - 1)

time: 60.4 us -> 60.1 us (level)
  no operation moved by 1% of the time
where the time goes in v7:
time: 60.1 us; the launch traced here: 59.9 us
  Pallas kernels  58.9 us (98%)
  local copies, waits for them, and re-layouts  0.97 us (2%)
    pallas_call x1, Pallas kernels, shards(): pl.pallas_call(functools.partial(kernel, sizes), out_shape=jax.ShapeDtype...  58.9 us

profile of v7, /device:TPU:0, one launch (start us, length us, event | category | flops | bytes accessed | tf_op | source)
XLA Modules:
  0.0 59.9 jit_solution(7814072854067769075)
XLA Ops:
  0.0 58.9 %shard_map.73 = f32[4,16,16,256]{3,2,1,0:T(8,128)S(1)} custom-call(f32[16,16,256]{2,1,0:T(8,128)} %courant.1, f32[16,16,256]{2,1,0:T(8,128)} %epsilon.1, f32[16,16,256]{2,1,0:T(8,128)} %delta.1, f32[2,2,2,16,16,256]{5,4,3,2,1,0:T(8,128)} %checkpoint.1, s32[3,4,512]{2,1,0:T(4,128)} %bitcast.1, f32[4,16,512]{2,1,0:T(8,128)} %weights.1, s32[16]{0:T(128)} %shifts.1), custom_call_target="tpu_custom_call" | custom-call | tf_op jit(solution)/shard_map/pallas_call | solution.py:617
  58.9 1.0 %copy.9 = f32[4,16,16,256]{3,2,1,0:T(8,128)} copy(f32[4,16,16,256]{3,2,1,0:T(8,128)S(1)} %shard_map.73) | data formatting | bytes 2097152
